TPU v7x, 128 devices: a whole 4x4x4 slice. The times are simulated.
128 devices in a mesh: dp: 8 (over z, core), dom: 16 (over y, x).
Axes of the slice: x: 4, y: 4, z: 4, core: 2. Of those that a mesh axis runs over, the one named last changes fastest.
Arguments:
- grad_out: bfloat16 [8, 48, 512, 256], P('dp', 'dom'), may hold values from -6 to 6
- pre_act: bfloat16 [8, 48, 512, 256], P('dp', 'dom'), may hold values from -6 to 6
- conv_weight: bfloat16 [27, 256, 256], replicated, may hold values from -0.078125 to 0.078125
- down_weight: bfloat16 [8, 128, 256], replicated, may hold values from -0.1875 to 0.1875
- fine_act: bfloat16 [8, 384, 512, 128], P('dp', 'dom'), may hold values from -6 to 6
- neighbours: int32 [8, 48, 27], P('dp', 'dom'), may hold values from -1 to 2, as said below
- octant_routes: int32 [8, 16, 3, 8], P('dp', 'dom'), may hold values from -1 to 23, as said below
Outputs:
- fine_grad: bfloat16 [8, 384, 512, 128], P('dp', 'dom')
- conv_weight_grad: float32 [6912, 256], P('dp')
- down_weight_grad: float32 [1024, 256], P('dp')
Inputs may be any that keep to these rules, and one draw needn't show every extreme that they name: `neighbours`: each device of a scene group has between half of 3 (rounded up) and 3 live slots, always the first ones, and some device of each scene group has all 3 live. A live slot's entry 13 is itself; entry 9(a+1)+3(b+1)+(c+1) is the slot, on the device a steps along dom, of the block displaced by (a, b, c) block edges within a slab of 3 x 3 positions, or -1 where that block is empty or outside the scene group; dead slots hold -1 in all 27 entries; the relation is symmetric. `octant_routes`: row (d, k) lists what device d sends to the device d + k - 1 along dom, taken cyclically: entries 8 s + o name octant o of slot s; each live slot's 8 octants stand together, in order, in exactly one row; live entries come first, then -1. A row holds at most 8 entries, and some row of the fullest device holds exactly 8. Dead slots are never named.
All inputs are finite; a program needn't handle non-finite values.
Results may differ from a plain program's by a relative error of at most 0.0065.
Values may be sent and summed in bfloat16 or wider, within the bound.
A program may use at most 128 MiB of HBM per device.

v0:
```python
import math

import jax
import jax.numpy as jnp
from jax import lax
from jax.sharding import PartitionSpec as P

BE = 8


def extended_2(block, sides, width):
    for axis, dim in sides:
        count = lax.axis_size(axis)
        forward = [(i, i + 1) for i in range(count - 1)]
        backward = [(target, source) for source, target in forward]
        low = lax.ppermute(
            lax.slice_in_dim(block, block.shape[dim] - width, None, axis=dim), axis, forward
        )
        high = lax.ppermute(lax.slice_in_dim(block, 0, width, axis=dim), axis, backward)
        block = jnp.concatenate([low, block, high], axis=dim)
    return block


def passed_along(value, axis, steps):
    count = lax.axis_size(axis)
    pairs = [(source, (source + steps) % count) for source in range(count)]
    return lax.ppermute(value, axis, pairs)


def pick_rows(source, slot_index):
    extended = jnp.concatenate([source, jnp.zeros_like(source[:1])], axis=0)
    return extended[jnp.where(slot_index < 0, source.shape[0], slot_index)]


def assemble(own_blocks, lower_faces, upper_faces, block_links):
    block_edge = own_blocks.shape[1]
    sources = (lower_faces, own_blocks, upper_faces)
    ranges = ((block_edge - 1, block_edge), (0, block_edge), (0, 1))
    parts_x = []
    for shift_x in range(3):
        parts_y = []
        for shift_y in range(3):
            parts_z = []
            for shift_z in range(3):
                links = block_links[:, 9 * shift_x + 3 * shift_y + shift_z]
                if shift_x == 1 and shift_y == 1 and (shift_z == 1):
                    portion = jnp.where(
                        (links >= 0)[:, None, None, None, None],
                        own_blocks,
                        jnp.zeros_like(own_blocks),
                    )
                else:
                    cut = sources[shift_x][
                        :,
                        :,
                        ranges[shift_y][0] : ranges[shift_y][1],
                        ranges[shift_z][0] : ranges[shift_z][1],
                    ]
                    portion = pick_rows(cut, links)
                parts_z.append(portion)
            parts_y.append(jnp.concatenate(parts_z, axis=3))
        parts_x.append(jnp.concatenate(parts_y, axis=2))
    return jnp.concatenate(parts_x, axis=1)


def correlate(grad_pad, act_pad, weight):
    block_edge = grad_pad.shape[1] - 2
    channels = grad_pad.shape[-1]
    count_blocks = grad_pad.shape[0]
    span = block_edge + 2

    def window(padded, start_x, start_y, start_z):
        return padded[
            :,
            start_x : start_x + block_edge,
            start_y : start_y + block_edge,
            start_z : start_z + block_edge,
        ].reshape(-1, channels)

    centre_grad = window(grad_pad, 1, 1, 1)
    slabs = [
        grad_pad[:, 1 - tap_x : 1 - tap_x + block_edge].reshape(-1, channels)
        for tap_x in (-1, 0, 1)
    ]
    input_grad = jnp.zeros(
        (count_blocks, block_edge, block_edge, block_edge, weight.shape[1]), jnp.float32
    )
    for tap_y in (-1, 0, 1):
        for tap_z in (-1, 0, 1):
            plane_sum = jnp.zeros((slabs[0].shape[0], weight.shape[1]), jnp.float32)
            for index_x in range(3):
                position = 9 * index_x + 3 * (tap_y + 1) + (tap_z + 1)
                plane_sum = plane_sum + lax.dot_general(
                    slabs[index_x],
                    weight[position],
                    (((1,), (1,)), ((), ())),
                    preferred_element_type=jnp.float32,
                )
            plane_sum = plane_sum.reshape(count_blocks, block_edge, span, span, weight.shape[1])
            input_grad = (
                input_grad
                + plane_sum[
                    :, :, 1 - tap_y : 1 - tap_y + block_edge, 1 - tap_z : 1 - tap_z + block_edge
                ]
            )
    weight_grads = []
    for position in range(27):
        tap_x = position // 9 - 1
        tap_y = position // 3 % 3 - 1
        tap_z = position % 3 - 1
        weight_grads.append(
            lax.dot_general(
                window(act_pad, 1 + tap_x, 1 + tap_y, 1 + tap_z),
                centre_grad,
                (((0,), (0,)), ((), ())),
                preferred_element_type=jnp.float32,
            )
        )
    return (input_grad.reshape(-1, weight.shape[1]), jnp.stack(weight_grads))


def split_octants(blocks):
    count_blocks = blocks.shape[0]
    half_edge = blocks.shape[1] // 2
    channels = blocks.shape[-1]
    parted = blocks.reshape(count_blocks, 2, half_edge, 2, half_edge, 2, half_edge, channels)
    parted = parted.transpose(0, 1, 3, 5, 2, 4, 6, 7)
    return parted.reshape(count_blocks * 8, half_edge * half_edge * half_edge, channels)


def body(grad_out, pre_act, conv_weight, down_weight, fine_act, neighbours, octant_routes):
    slot_total = grad_out.shape[1]
    voxels = grad_out.shape[2]
    channels = grad_out.shape[3]
    grad_blocks = grad_out[0].reshape(slot_total, BE, BE, BE, channels)
    act_blocks = jnp.maximum(pre_act[0], 0).reshape(slot_total, BE, BE, BE, channels)
    block_links = neighbours[0]
    faces = jnp.stack(
        [
            jnp.stack([grad_blocks[:, 0], grad_blocks[:, BE - 1]]),
            jnp.stack([act_blocks[:, 0], act_blocks[:, BE - 1]]),
        ]
    )
    widened = extended_2(faces, (("dom", 1),), 1)
    lower_faces = widened[:, 0][:, :, None]
    upper_faces = widened[:, 3][:, :, None]
    grad_pad = assemble(grad_blocks, lower_faces[0], upper_faces[0], block_links)
    act_pad = assemble(act_blocks, lower_faces[1], upper_faces[1], block_links)
    input_grad, conv_part = correlate(grad_pad, act_pad, conv_weight)
    grad_in = jnp.where(pre_act[0].reshape(-1, channels) > 0, input_grad, 0.0).astype(jnp.bfloat16)
    octants = split_octants(grad_in.reshape(slot_total, BE, BE, BE, channels))
    octant_voxels = octants.shape[1]
    peer_places = octant_routes.shape[-1]
    outgoing = pick_rows(octants, octant_routes[0, 0].reshape(-1)).reshape(
        3, peer_places, octant_voxels, channels
    )
    from_upper = passed_along(outgoing[0], "dom", -1)
    from_lower = passed_along(outgoing[2], "dom", 1)
    arrived = jnp.stack([from_upper, outgoing[1], from_lower])
    octant_grad = arrived.reshape(-1, octant_voxels, channels)
    fine_split = fine_act[0].reshape(fine_act.shape[1], 8, octant_voxels, fine_act.shape[3])
    fine_grad = jnp.einsum(
        "fcj,qij->fqci", octant_grad, down_weight, preferred_element_type=jnp.float32
    )
    fine_grad = fine_grad.astype(jnp.bfloat16).reshape(fine_act.shape)
    down_part = jnp.einsum(
        "fqci,fcj->qij", fine_split, octant_grad, preferred_element_type=jnp.float32
    )
    conv_part = conv_part.reshape(-1, channels)
    down_part = down_part.reshape(-1, channels)
    factor = 1.0 / math.sqrt(lax.axis_size("dp") * lax.axis_size("dom") * slot_total * voxels)
    conv_sum, down_sum = lax.psum((conv_part, down_part), ("dp", "dom"))
    data_index = lax.axis_index("dp")
    data_length = lax.axis_size("dp")
    conv_rows = conv_sum.shape[0] // data_length
    down_rows = down_sum.shape[0] // data_length
    conv_sum = lax.dynamic_slice_in_dim(conv_sum, data_index * conv_rows, conv_rows, 0)
    down_sum = lax.dynamic_slice_in_dim(down_sum, data_index * down_rows, down_rows, 0)
    return (fine_grad, conv_sum * factor, down_sum * factor)


def solution(mesh):
    return jax.shard_map(
        body,
        mesh=mesh,
        in_specs=(
            P("dp", "dom", None, None),
            P("dp", "dom", None, None),
            P(),
            P(),
            P("dp", "dom", None, None),
            P("dp", "dom", None),
            P("dp", "dom", None, None),
        ),
        out_specs=(P("dp", "dom", None, None), P("dp", None), P("dp", None)),
        check_vma=False,
    )
```

profile of v0, /device:TPU:0, one launch (start us, length us, event | category | flops | bytes accessed | tf_op | source)
XLA Modules:
  0.0 578.6 jit_solution(6028109228786155861)
XLA Ops:
  11.9 5.2 collective-permute-start.1
  44.6 2.7 broadcast_select_fusion
  58.2 2.2 gather_fusion.1
  60.4 3.7 maximum_maximum_fusion.2
  64.1 3.6 reshape.154
  67.7 2.2 gt.12
  84.5 2.2 gather_fusion.37
  98.3 4.9 maximum_maximum_fusion.4
  130.5 2.2 gather_fusion.12
  134.7 6.3 %fusion.6 = bf16[3,8,10,10,256]{4,3,2,1,0:T(8,128)(2,1)} fusion(bf16[3,1,1,1,256]{4,3,2,1,0:T(2,128)(2,1)} %copy.77, bf16[3,8,1,1,256]{4,3,2,1,0:T(2,128)(2,1)} %copy.68, bf16[3,1,1,8,256]{4,3,2,1,0:T(8,128)(2,1)S(1)} %bitcast.643, bf16[3,1,1,1,256]{4,3,2,1,0:T(2,128)(2,1)} %copy.76, bf16[3,1,8,1,256]{4,3,2,1,0:T(2,128)(2,1)} %copy.75, ...), kind=kLoop, calls=%fused_computation.93 | loop fusion | flops 22118400 | bytes 2611200 | tf_op jit(solution)/shard_map/concatenate | solution.py:63
  141.1 3.5 reshape.153
  144.6 3.3 fusion.75
  148.0 2.9 fusion.79
  150.8 2.9 fusion.83
  153.7 2.9 fusion.87
  156.7 2.9 fusion.91
  159.5 2.9 fusion.95
  162.4 2.9 fusion.99
  165.3 2.9 fusion.103
  168.2 2.9 fusion.107
  193.9 2.2 gather_fusion.21
  198.1 5.7 fusion.1
  203.9 3.5 reshape.155
  207.4 2.7 convolution_add_fusion.1
  210.2 2.9 convolution_add_fusion
  213.0 4.4 reshape.164
  217.4 2.7 convolution_add_fusion.3
  220.2 2.9 convolution_add_fusion.2
  223.0 4.2 reshape.163
  227.2 2.7 convolution_add_fusion.5
  230.0 2.9 convolution_add_fusion.4
  232.9 4.2 reshape.162
  237.1 2.7 convolution_add_fusion.7
  239.8 2.9 convolution_add_fusion.6
  242.7 4.2 reshape.161
  246.9 2.7 convolution_add_fusion.9
  249.7 2.9 convolution_add_fusion.8
  252.6 4.2 reshape.160
  256.8 2.7 convolution_add_fusion.11
  259.5 2.9 convolution_add_fusion.10
  262.4 4.2 reshape.159
  266.6 2.7 convolution_add_fusion.13
  269.4 2.9 convolution_add_fusion.12
  272.2 4.2 reshape.158
  276.5 2.7 convolution_add_fusion.15
  279.2 2.9 convolution_add_fusion.14
  282.1 4.2 reshape.157
  286.3 2.7 convolution_add_fusion.17
  289.0 2.9 convolution_add_fusion.16
  291.9 4.2 reshape.156
  296.1 10.5 %slice_add_fusion = bf16[3,8,8,8,256]{4,3,2,1,0:T(8,128)(2,1)} fusion(f32[3,8,10,10,256]{4,3,2,1,0:T(8,128)} %reshape.164, f32[3,8,10,10,256]{4,3,2,1,0:T(8,128)} %reshape.163, f32[3,8,10,10,256]{4,3,2,1,0:T(8,128)} %reshape.162, f32[3,8,10,10,256]{4,3,2,1,0:T(8,128)} %reshape.161, f32[3,8,10,10,256]{4,3,2,1,0:T(8,128)} %reshape.160, ...), kind=kLoop, calls=%fused_computation.111 | loop fusion | flops 3538944 | bytes 14942208 | tf_op jit(solution)/shard_map/add | solution.py:101
  306.6 2.4 reshape.165
  309.0 2.8 fusion.38
  311.7 2.3 reshape.166
  316.1 2.8 gather_fusion.26
  321.8 4.8 collective-permute-start.2
  335.2 2.2 gather_fusion.31
  347.9 2.6 maximum_maximum_fusion
  362.5 2.9 copy-done.15
  374.0 2.2 gather_fusion.48
  384.8 7.1 %maximum_maximum_fusion.1 = bf16[3,9,10,10,256]{4,3,2,1,0:T(8,128)(2,1)S(1)} fusion(bf16[3,1,1,1,256]{4,3,2,1,0:T(2,128)(2,1)} %copy.108, bf16[3,1,1,8,256]{4,3,2,1,0:T(8,128)(2,1)} %bitcast.621, bf16[3,1,1,1,256]{4,3,2,1,0:T(2,128)(2,1)} %copy.107, bf16[3,1,8,1,256]{4,3,2,1,0:T(2,128)(2,1)} %copy.106, bf16[3,1,8,8,256]{4,3,2,1,0:T(8,128)(2,1)} %bitcast.618, ...), kind=kLoop, calls=%fused_computation.73 | loop fusion | flops 24883200 | bytes 2764800 | tf_op jit(solution)/shard_map/concatenate | solution.py:63
  403.5 2.3 fusion.186
  405.9 4.0 convolution_convert_fusion
  409.9 158.0 %all-reduce.56.cloned.1.call-done = (f32[6912,256]{1,0:T(8,128)}, f32[1024,256]{1,0:T(8,128)}) async-done(((f32[6912,256]{1,0:T(8,128)}, f32[1024,256]{1,0:T(8,128)}), (f32[6912,256]{1,0:T(8,128)}, f32[1024,256]{1,0:T(8,128)})) %all-reduce.56.cloned.1.call-update) | async-done | bytes 8126480 | tf_op jit(solution)/shard_map/psum | solution.py:172
  (338 shorter events, 191.5 us)
Async XLA Ops:
  7.2 396.4 %copy-start = (bf16[1,24,512,128]{3,2,1,0:T(8,128)(2,1)S(1)}, bf16[1,24,512,128]{3,2,1,0:T(8,128)(2,1)}, u32[]{:S(2)}) copy-start(bf16[1,24,512,128]{3,2,1,0:T(8,128)(2,1)} %param.11) | copy-start | bytes 9437188
  7.2 11.4 %copy-start.40 = (s32[1,3,27]{2,0,1:T(1,128)S(1)}, s32[1,3,27]{2,0,1:T(1,128)}, u32[]{:S(2)}) copy-start(s32[1,3,27]{2,0,1:T(1,128)} %param.12) | copy-start | bytes 976
  7.2 560.7 %all-reduce.56.cloned.1.call-start = ((), (), s32[]{:S(2)}) async-start(), calls=%async_computation | async-start | bytes 16252928 | tf_op jit(solution)/shard_map/psum | solution.py:172
  7.2 9.9 %copy-start.16 = (bf16[1,3,512,256]{3,2,1,0:T(8,128)(2,1)S(1)}, bf16[1,3,512,256]{3,2,1,0:T(8,128)(2,1)}, u32[]{:S(2)}) copy-start(bf16[1,3,512,256]{3,2,1,0:T(8,128)(2,1)} %param.7) | copy-start | bytes 2359300
  8.4 13.1 %copy-start.18 = (bf16[1,3,512,256]{3,2,1,0:T(8,128)(2,1)S(1)}, bf16[1,3,512,256]{3,2,1,0:T(8,128)(2,1)}, u32[]{:S(2)}) copy-start(bf16[1,3,512,256]{3,2,1,0:T(8,128)(2,1)} %param.8) | copy-start | bytes 2359300
  9.7 14.1 %copy-start.14 = (bf16[1,3,512,256]{3,2,1,0:T(8,128)(2,1)}, bf16[1,3,512,256]{3,2,1,0:T(8,128)(2,1)S(1)}, u32[]{:S(2)}) copy-start(bf16[1,3,512,256]{3,2,1,0:T(8,128)(2,1)S(1)} %broadcast_maximum_fusion) | copy-start | bytes 2359300
  10.6 93.8 %collective-permute-start = (bf16[2,1,3,8,8,256]{5,4,3,2,1,0:T(8,128)(2,1)}, bf16[2,1,3,8,8,256]{5,4,3,2,1,0:T(8,128)(2,1)}, u32[]{:S(2)}, u32[]{:S(2)}) collective-permute-start(bf16[2,1,3,8,8,256]{5,4,3,2,1,0:T(8,128)(2,1)} %get-tuple-element.57), channel_id=1, source_target_pairs={{1,0},{2,1},{3,2},{4,3},{5,4},{6,5},{7,6},{8,7},{9,8},{10,9},{11,1... | collective-permute-start | bytes 589832 | tf_op jit(solution)/shard_map/ppermute | solution.py:19
  11.9 96.6 %collective-permute-start.1 = (bf16[2,1,3,8,8,256]{5,4,3,2,1,0:T(8,128)(2,1)}, bf16[2,1,3,8,8,256]{5,4,3,2,1,0:T(8,128)(2,1)}, u32[]{:S(2)}, u32[]{:S(2)}) collective-permute-start(bf16[2,1,3,8,8,256]{5,4,3,2,1,0:T(8,128)(2,1)} %get-tuple-element.56), channel_id=1, source_target_pairs={{0,1},{1,2},{2,3},{3,4},{4,5},{5,6},{6,7},{7,8},{8,9},{9,10},{10,1... | collective-permute-start | bytes 589832 | tf_op jit(solution)/shard_map/ppermute | solution.py:16
  37.7 1.2 copy-start.34
  39.9 20.4 %copy-start.20 = (bf16[3,8,8,1,256]{4,3,2,1,0:T(2,128)(2,1)}, bf16[3,8,8,1,256]{4,3,2,1,0:T(2,128)(2,1)S(1)}, u32[]{:S(2)}) copy-start(bf16[3,8,8,1,256]{4,3,2,1,0:T(2,128)(2,1)S(1)} %copy.66) | copy-start | bytes 294916
  49.7 18.0 %copy-start.21 = (bf16[3,8,8,1,256]{4,3,2,1,0:T(2,128)(2,1)}, bf16[3,8,8,1,256]{4,3,2,1,0:T(2,128)(2,1)S(1)}, u32[]{:S(2)}) copy-start(bf16[3,8,8,1,256]{4,3,2,1,0:T(2,128)(2,1)S(1)} %copy.65) | copy-start | bytes 294916
  64.1 12.9 %copy-start.28 = (bf16[3,8,8,1,256]{4,3,2,1,0:T(2,128)(2,1)S(1)}, bf16[3,8,8,1,256]{4,3,2,1,0:T(2,128)(2,1)}, u32[]{:S(2)}) copy-start(bf16[3,8,8,1,256]{4,3,2,1,0:T(2,128)(2,1)} %get-tuple-element.40) | copy-start | bytes 294916
  89.5 13.7 %copy-start.29 = (bf16[3,8,1,1,256]{4,3,2,1,0:T(2,128)(2,1)}, bf16[3,8,1,1,256]{4,3,2,1,0:T(2,128)(2,1)S(1)}, u32[]{:S(2)}) copy-start(bf16[3,8,1,1,256]{4,3,2,1,0:T(2,128)(2,1)S(1)} %copy.93) | copy-start | bytes 36868
  98.2 5.0 copy-start.37
  98.2 5.0 copy-start.38
  98.2 5.6 copy-start.35
  98.2 5.6 copy-start.36
  144.6 3.3 copy-start.10
  168.2 2.9 copy-start.27
  168.2 5.4 copy-start.26
  168.2 8.0 %copy-start.33 = (bf16[3,1,1,1,256]{4,3,2,0,1:T(2,128)(2,1)S(1)}, bf16[3,1,1,1,256]{4,3,2,0,1:T(2,128)(2,1)}, u32[]{:S(2)}) copy-start(bf16[3,1,1,1,256]{4,3,2,0,1:T(2,128)(2,1)} %get-tuple-element.79) | copy-start | bytes 4612
  168.2 10.4 %copy-start.30 = (bf16[3,1,1,8,256]{4,3,2,0,1:T(8,128)(2,1)S(1)}, bf16[3,1,1,8,256]{4,3,2,0,1:T(8,128)(2,1)}, u32[]{:S(2)}) copy-start(bf16[3,1,1,8,256]{4,3,2,0,1:T(8,128)(2,1)} %get-tuple-element.83) | copy-start | bytes 36868
  207.4 2.7 copy-start.1
  217.4 2.8 copy-start.2
  227.2 2.8 copy-start.3
  237.1 2.8 copy-start.4
  246.9 2.8 copy-start.5
  256.8 2.7 copy-start.6
  266.6 2.7 copy-start.7
  276.5 2.7 copy-start.8
  286.3 2.7 copy-start.9
  314.0 12.6 %copy-start.32 = (bf16[3,1,1,1,256]{4,3,2,0,1:T(2,128)(2,1)S(1)}, bf16[3,1,1,1,256]{4,3,2,0,1:T(2,128)(2,1)}, u32[]{:S(2)}) copy-start(bf16[3,1,1,1,256]{4,3,2,0,1:T(2,128)(2,1)} %get-tuple-element.71) | copy-start | bytes 4612
  320.8 81.5 %collective-permute-start.3 = (bf16[8,64,256]{2,1,0:T(8,128)(2,1)}, bf16[8,64,256]{2,1,0:T(8,128)(2,1)}, u32[]{:S(2)}, u32[]{:S(2)}) collective-permute-start(bf16[8,64,256]{2,1,0:T(8,128)(2,1)} %get-tuple-element.43), channel_id=1, source_target_pairs={{0,1},{1,2},{2,3},{3,4},{4,5},{5,6},{6,7},{7,8},{8,9},{9,10},{10,1... | collective-permute-start | bytes 786440 | tf_op jit(solution)/shard_map/ppermute | solution.py:27
  321.8 80.6 %collective-permute-start.2 = (bf16[8,64,256]{2,1,0:T(8,128)(2,1)}, bf16[8,64,256]{2,1,0:T(8,128)(2,1)}, u32[]{:S(2)}, u32[]{:S(2)}) collective-permute-start(bf16[8,64,256]{2,1,0:T(8,128)(2,1)} %get-tuple-element.41), channel_id=1, source_target_pairs={{0,15},{1,0},{2,1},{3,2},{4,3},{5,4},{6,5},{7,6},{8,7},{9,8},{10,9... | collective-permute-start | bytes 786440 | tf_op jit(solution)/shard_map/ppermute | solution.py:27
  346.0 4.5 copy-start.11
  354.2 1.5 copy-start.24
  356.6 1.1 copy-start.13
  357.7 1.1 copy-start.17
  357.7 1.4 copy-start.19
  357.7 1.4 copy-start.39
  359.6 1.5 copy-start.23
  362.0 3.4 copy-start.31
  362.5 2.9 copy-start.15
  384.8 7.1 %copy-start.12 = (bf16[3,8,8,8,256]{4,3,2,1,0:T(8,128)(2,1)S(1)}, bf16[3,8,8,8,256]{4,3,2,1,0:T(8,128)(2,1)}, u32[]{:S(2)}) copy-start(bf16[3,8,8,8,256]{4,3,2,1,0:T(8,128)(2,1)} %get-tuple-element.95) | copy-start | bytes 2359300
  401.2 1.2 copy-start.25
  403.5 2.4 copy-start.22
Sparse Core Ops, SparseCore 0:
  406.0 161.7 all-reduce.55
where the time goes:
time: 588 us; the launch traced here: 579 us
  local copies, waits for them, and re-layouts  214 us (36%)
  waiting for transfers between devices  158 us (27%)
  matrix products  102 us (17%)
  other arithmetic  76.9 us (13%)
  between operations  15 us (3%)
  starting transfers between devices  12.3 us (2%)
    psum x1, waiting for transfers between devices, body(): conv_sum, down_sum = lax.psum((conv_part, down_part), ('dp', 'dom'))  158 us
    gather x89, local copies, waits for them, and re-layouts, pick_rows(): return extended[jnp.where(slot_index < 0, source.shape[0], slot_index)]  98 us
    dot_general x27, matrix products, correlate(): lax.dot_general(slabs[index_x], weight[position], (((1,), (1,)), ((), ())...  76.9 us
    reshape x9, local copies, waits for them, and re-layouts, correlate(): plane_sum.reshape(count_blocks, block_edge, span, span, weight.shape[1])  38.1 us
    unnamed x155, local copies, waits for them, and re-layouts  26.8 us
    concatenate x4, other arithmetic, assemble(): return jnp.concatenate(parts_x, axis=1)  21.7 us
    dot_general x27, matrix products, correlate(): lax.dot_general(window(act_pad, 1 + tap_x, 1 + tap_y, 1 + tap_z), centre_...  19 us
    gather x14, other arithmetic, pick_rows(): return extended[jnp.where(slot_index < 0, source.shape[0], slot_index)]  16.2 us
  transfers between devices with their start and end apart: 5, of which 1 were waited for; matrix products, arithmetic and copies ran while one was open for 28% of the time, Pallas kernels for 0%

commit v1 on v0

v1 whole, which is shorter than its diff:
```python
import math

import jax
import jax.numpy as jnp
from jax import lax
from jax.experimental import pallas as pl
from jax.experimental.pallas import tpu as pltpu
from jax.sharding import PartitionSpec as P

MESH = pl.DeviceIdType.MESH
BF = jnp.bfloat16
F32 = jnp.float32
CAP = 3
GROUPS = 4
ORDERS = ("zxy", "xyz", "yzx", "xyz")


def dot_nt(a, b):
    return lax.dot_general(a, b, (((1,), (1,)), ((), ())), preferred_element_type=F32)


def dot_nn(a, b):
    return lax.dot_general(a, b, (((1,), (0,)), ((), ())), preferred_element_type=F32)


def kernel(
    links, routes, g_hbm, p_hbm, w_hbm, dw_hbm, fine_hbm,
    fg_hbm, red_hbm,
    g, p, face, gsh, ash, gt, w, dw, fine, fg, acc, octs, out, octin, ot,
    part, rcore, racc, r1, a1, r2, a2, r3, red,
    load_sem, halo_s, halo_r, oct_s, oct_r, red_s, red_r, fg_sem,
):
    dp = lax.axis_index("dp")
    dom = lax.axis_index("dom")
    zc, cc = dp // 2, dp % 2
    yc, xc = dom // 4, dom % 4
    coord = {"z": zc, "x": xc, "y": yc}

    def dev(axis, to):
        if axis == "z":
            return (to * 2 + cc, dom)
        if axis == "x":
            return (dp, yc * 4 + to)
        return (dp, to * 4 + xc)

    def ring(axis, off):
        return lax.rem(coord[axis] + off, 4)

    partner = (zc * 2 + (1 - cc), dom)
    nxt = (dp, lax.rem(dom + 1, 16))
    prv = (dp, lax.rem(dom + 15, 16))

    barrier = pltpu.get_barrier_semaphore()
    peers = [partner, nxt, prv]
    for axis in "xyz":
        for off in (1, 2, 3):
            peers.append(dev(axis, ring(axis, off)))
    for peer in peers:
        pl.semaphore_signal(barrier, inc=1, device_id=peer, device_id_type=MESH)

    loads = []
    for i, (src, dst) in enumerate(
        ((g_hbm, g.at[0:CAP]), (p_hbm, p.at[0:CAP]), (w_hbm, w), (fine_hbm, fine), (dw_hbm, dw))
    ):
        c = pltpu.make_async_copy(src, dst, load_sem.at[i])
        c.start()
        loads.append(c)
    g[CAP] = jnp.zeros(g.shape[1:], BF)
    p[CAP] = jnp.zeros(p.shape[1:], BF)
    for i in range(4):
        face[i, CAP] = jnp.zeros(face.shape[2:], BF)
    octs[24] = jnp.zeros(octs.shape[1:], BF)
    for s in range(8):
        part[3, s // 2, s % 2, 3, 2:4] = jnp.zeros((2, 16, 256), BF)
    loads[0].wait()
    loads[1].wait()
    pl.semaphore_wait(barrier, len(peers))

    def rcopy(src, dst, ss, rs, to):
        return pltpu.make_async_remote_copy(
            src_ref=src, dst_ref=dst, send_sem=ss, recv_sem=rs, device_id=to, device_id_type=MESH
        )

    halos = []
    for i, (src, to) in enumerate(
        (
            (p.at[0:CAP, 7], nxt),
            (p.at[0:CAP, 0], prv),
            (g.at[0:CAP, 7], nxt),
            (g.at[0:CAP, 0], prv),
        )
    ):
        c = rcopy(src, face.at[i, 0:CAP], halo_s.at[i], halo_r.at[i], to)
        c.start()
        halos.append(c)

    zi = lax.broadcasted_iota(jnp.int32, (10, 8, 256), 1)

    def expand(load, a, blk, plane, dst, relu):
        def slot(b, c):
            n = links[blk, 9 * (a + 1) + 3 * (b + 1) + (c + 1)]
            return jnp.where(n < 0, CAP, n)

        cols = []
        for c in (-1, 0, 1):
            low = load(slot(-1, c), pl.ds(48, 16)).astype(F32)[8:16]
            mid = load(slot(0, c), pl.ds(0, 64)).astype(F32)
            high = load(slot(1, c), pl.ds(0, 16)).astype(F32)[0:8]
            col = jnp.concatenate([low, mid, high], axis=0)
            if relu:
                col = jnp.maximum(col, 0.0)
            cols.append(col.reshape(10, 8, 256))
        shifted = (
            pltpu.roll(jnp.where(zi == 7, cols[0], cols[1]), 1, 1),
            cols[1],
            pltpu.roll(jnp.where(zi == 0, cols[2], cols[1]), 7, 1),
        )
        rows = pl.ds(pl.multiple_of(blk * 64, 64), 64)
        for ty in range(3):
            for tz in range(3):
                dst[3 * ty + tz, plane, rows] = shifted[tz][ty : ty + 8].reshape(64, 256).astype(BF)

    def inner(n, _):
        blk, x = n // 8, n % 8
        expand(lambda s, r: p[s, x, r], 0, blk, x + 1, ash, True)
        expand(lambda s, r: g[s, x, r], 0, blk, x + 1, gsh, False)
        return 0

    lax.fori_loop(0, CAP * 8, inner, 0)

    def transpose_plane(x, _):
        cols = pl.ds(pl.multiple_of(x * 2, 2), 2)
        gt[:, pl.ds(pl.multiple_of(x * 384, 384), 384)] = (
            gsh[4, pl.ds(1 + 2 * x, 2)].reshape(384, 256).T
        )
        return 0

    lax.fori_loop(0, 4, transpose_plane, 0)

    def tap(t, _):
        tx, tyz = t // 9, t % 9
        rows = ash[tyz, pl.ds(tx, 8)].reshape(1536, 256)
        grad = dot_nn(gt[...], rows).T.astype(BF)
        for i in range(8):
            m = t * 8 + i
            k, r = m // 27, m % 27
            q8 = r % 8
            part[r // 8, k // 2, k % 2, q8 // 2, pl.ds((q8 % 2) * 2, 2)] = grad[
                32 * i : 32 * i + 32
            ].reshape(2, 16, 256)
        return 0

    lax.fori_loop(9, 18, tap, 0)

    for c in halos:
        c.wait_recv()

    def outer(blk, _):
        expand(lambda s, r: face[0, s, r], -1, blk, 0, ash, True)
        expand(lambda s, r: face[1, s, r], 1, blk, 9, ash, True)
        expand(lambda s, r: face[2, s, r], -1, blk, 0, gsh, False)
        expand(lambda s, r: face[3, s, r], 1, blk, 9, gsh, False)
        return 0

    lax.fori_loop(0, CAP, outer, 0)
    lax.fori_loop(0, 9, tap, 0)
    lax.fori_loop(18, 27, tap, 0)

    flights = []

    def launch(grp, base, axis, src_of, dst_of):
        copies = []
        for off in (1, 2, 3):
            to = ring(axis, off)
            i = base + off - 1
            c = rcopy(
                src_of(to), dst_of(off - 1), red_s.at[grp, i], red_r.at[grp, i], dev(axis, to)
            )
            c.start()
            copies.append(c)
        flights.extend(copies)
        return copies

    def cut(ref, dims, axis, at):
        return ref.at[tuple(at if d == axis else slice(None) for d in dims)]

    class Group:
        def __init__(self, grp):
            self.grp = grp
            self.order = ORDERS[grp]
            self.done = 0

        def start(self):
            grp = self.grp
            self.copies = [
                rcopy(
                    part.at[grp, :, 1 - cc], rcore.at[grp], red_s.at[grp, 0], red_r.at[grp, 0],
                    partner,
                )
            ]
            self.copies[0].start()
            flights.extend(self.copies)

        def step(self):
            grp, order, n = self.grp, self.order, self.done
            self.done += 1
            for c in self.copies:
                c.wait_recv()
            if n == 0:
                for z in range(4):
                    racc[grp, z] = (
                        part[grp, z, cc].astype(F32) + rcore[grp, z].astype(F32)
                    ).astype(BF)
                src = racc.at[grp]
                dims = "zxy"
                self.copies = launch(
                    grp, 1, order[0], lambda to: cut(src, dims, order[0], to),
                    lambda s: r1.at[grp, s],
                )
                return
            if n == 1:
                mine = cut(racc.at[grp], "zxy", order[0], coord[order[0]])
                total = mine[...].astype(F32)
                for s in range(3):
                    total = total + r1[grp, s].astype(F32)
                a1[grp] = total.astype(BF)
                src = a1.at[grp]
                dims = "zxy".replace(order[0], "")
                self.copies = launch(
                    grp, 4, order[1], lambda to: cut(src, dims, order[1], to),
                    lambda s: r2.at[grp, s],
                )
                return
            if n == 2:
                dims = "zxy".replace(order[0], "")
                mine = cut(a1.at[grp], dims, order[1], coord[order[1]])
                total = mine[...].astype(F32)
                for s in range(3):
                    total = total + r2[grp, s].astype(F32)
                a2[grp] = total.astype(BF)
                src = a2.at[grp]
                self.copies = launch(
                    grp, 7, order[2], lambda to: src.at[to], lambda s: r3.at[grp, s]
                )
                return
            first, second = ("y", "x") if grp % 2 == 0 else ("x", "y")
            if n == 3:
                total = a2[grp, coord[order[2]]].astype(F32)
                for s in range(3):
                    total = total + r3[grp, s].astype(F32)
                red[grp, xc, yc] = total.astype(BF)
                spot = red.at[grp, xc, yc]
                self.copies = launch(grp, 10, first, lambda to: spot, lambda s: spot)
                return
            if n == 4:
                spot = cut(red.at[grp], "xy", second, coord[second])
                self.copies = launch(grp, 13, second, lambda to: spot, lambda s: spot)
                return

    groups = [Group(i) for i in range(GROUPS)]
    early, late = groups[:3], groups[3:]

    def step(some):
        for one in some:
            one.step()

    for one in early:
        one.start()
    loads[2].wait()

    def input_grad(half):
        def taps(tyz, _):
            lhs = jnp.concatenate(
                [gsh[8 - tyz, pl.ds(2 - i + 4 * half, 4)].reshape(768, 256) for i in range(3)],
                axis=1,
            )
            rhs = jnp.concatenate([w[9 * i + tyz] for i in range(3)], axis=1)
            res = dot_nt(lhs, rhs)
            acc[half] += res
            return 0

        acc[half] = jnp.zeros((768, 256), F32)
        lax.fori_loop(0, 9, taps, 0)

    lower = lax.broadcasted_iota(jnp.int32, (2, 8, 256), 1) < 4

    def octants(half):
        def plane(n, _):
            cx, blk = n // CAP, n % CAP
            val = acc[half, pl.ds(pl.multiple_of(n * 64, 64), 64)]
            pre = p[blk, 4 * half + cx].astype(F32)
            val = jnp.where(pre > 0.0, val, 0.0).reshape(2, 2, 2, 8, 256)
            for oy in range(2):
                even, odd = val[oy, :, 0], val[oy, :, 1]
                first = jnp.where(lower, even, pltpu.roll(odd, 4, 1))
                second = jnp.where(lower, pltpu.roll(even, 4, 1), odd)
                rows = pl.ds(pl.multiple_of(cx * 16, 16), 16)
                slot = blk * 8 + 4 * half + 2 * oy
                octs[slot, rows] = first.reshape(16, 256).astype(BF)
                octs[slot + 1, rows] = second.reshape(16, 256).astype(BF)
            return 0

        lax.fori_loop(0, 4 * CAP, plane, 0)

    input_grad(0)
    step(early)
    octants(0)
    input_grad(1)
    step(early)
    octants(1)

    def route(k):
        def place(j, _):
            e = routes[k, j]
            val = octs[jnp.where(e < 0, 24, e)]
            if k == 1:
                octin[8 + j] = val
            else:
                out[k // 2, j] = val
            return 0

        lax.fori_loop(0, 8, place, 0)

    route(0)
    passing = [rcopy(out.at[0], octin.at[0:8], oct_s.at[0], oct_r.at[0], prv)]
    passing[0].start()
    route(2)
    passing.append(rcopy(out.at[1], octin.at[16:24], oct_s.at[1], oct_r.at[1], nxt))
    passing[1].start()
    step(early)
    route(1)
    loads[3].wait()
    loads[4].wait()
    step(early)
    for c in passing:
        c.wait_recv()

    def turn(i, _):
        ot[:, pl.ds(pl.multiple_of(i * 384, 384), 384)] = (
            octin[pl.ds(6 * i, 6)].reshape(384, 256).T
        )
        return 0

    lax.fori_loop(0, 4, turn, 0)

    def down(i, _):
        rows = jnp.concatenate(
            [fine[:, 2 * i].reshape(1536, 128), fine[:, 2 * i + 1].reshape(1536, 128)], axis=1
        )
        grad = dot_nn(ot[...], rows).T.astype(BF)
        for c in range(2):
            one = grad[128 * c : 128 * c + 128]
            part[3, i, c, 1, 2:4] = one[0:32].reshape(2, 16, 256)
            part[3, i, c, 2] = one[32:96].reshape(4, 16, 256)
            part[3, i, c, 3, 0:2] = one[96:128].reshape(2, 16, 256)
        return 0

    lax.fori_loop(0, 4, down, 0)
    late[0].start()
    step(early)

    def fine_grad(i, _):
        at = pl.ds(4 * i, 4)
        res = dot_nt(octin[at].reshape(256, 256), dw[...]).astype(BF)
        for q in range(8):
            fg[at, q] = res[:, 128 * q : 128 * q + 128].reshape(4, 64, 128)
        return 0

    puts = []
    for i in range(3):
        lax.fori_loop(2 * i, 2 * i + 2, fine_grad, 0)
        c = pltpu.make_async_copy(
            fg.at[8 * i : 8 * i + 8], fg_hbm.at[8 * i : 8 * i + 8], fg_sem.at[i]
        )
        c.start()
        puts.append(c)
        step(late)
    step(late)
    step(late)
    for one in groups:
        for c in one.copies:
            c.wait_recv()
    c = pltpu.make_async_copy(red, red_hbm, fg_sem.at[3])
    c.start()
    puts.append(c)
    for c in halos + passing + flights:
        c.wait_send()
    for c in puts:
        c.wait()


def body(grad_out, pre_act, conv_weight, down_weight, fine_act, neighbours, octant_routes):
    slots, voxels, channels = grad_out.shape[1:]
    any_space = pl.BlockSpec(memory_space=pl.ANY)
    smem = pl.BlockSpec(memory_space=pltpu.SMEM)
    V = pltpu.VMEM
    fg, red = pl.pallas_call(
        kernel,
        out_shape=(
            jax.ShapeDtypeStruct((24, 8, 64, 128), BF),
            jax.ShapeDtypeStruct((GROUPS, 4, 4, 16, 256), BF),
        ),
        in_specs=[smem, smem] + [any_space] * 5,
        out_specs=(any_space, any_space),
        scratch_shapes=[
            V((CAP + 1, 8, 64, 256), BF),
            V((CAP + 1, 8, 64, 256), BF),
            V((4, CAP + 1, 64, 256), BF),
            V((9, 10, 192, 256), BF),
            V((9, 10, 192, 256), BF),
            V((256, 1536), BF),
            V((27, 256, 256), BF),
            V((1024, 256), BF),
            V((24, 8, 64, 128), BF),
            V((24, 8, 64, 128), BF),
            V((2, 768, 256), F32),
            V((25, 64, 256), BF),
            V((2, 8, 64, 256), BF),
            V((24, 64, 256), BF),
            V((256, 1536), BF),
            V((GROUPS, 4, 2, 4, 4, 16, 256), BF),
            V((GROUPS, 4, 4, 4, 16, 256), BF),
            V((GROUPS, 4, 4, 4, 16, 256), BF),
            V((GROUPS, 3, 4, 4, 16, 256), BF),
            V((GROUPS, 4, 4, 16, 256), BF),
            V((GROUPS, 3, 4, 16, 256), BF),
            V((GROUPS, 4, 16, 256), BF),
            V((GROUPS, 3, 16, 256), BF),
            V((GROUPS, 4, 4, 16, 256), BF),
            pltpu.SemaphoreType.DMA((5,)),
            pltpu.SemaphoreType.DMA((4,)),
            pltpu.SemaphoreType.DMA((4,)),
            pltpu.SemaphoreType.DMA((2,)),
            pltpu.SemaphoreType.DMA((2,)),
            pltpu.SemaphoreType.DMA((GROUPS, 16)),
            pltpu.SemaphoreType.DMA((GROUPS, 16)),
            pltpu.SemaphoreType.DMA((4,)),
        ],
        compiler_params=pltpu.CompilerParams(
            collective_id=0, has_side_effects=True, vmem_limit_bytes=60 * 1024 * 1024
        ),
        name="backward",
    )(
        neighbours[0],
        octant_routes[0, 0],
        grad_out[0].reshape(slots, 8, 64, channels),
        pre_act[0].reshape(slots, 8, 64, channels),
        conv_weight,
        down_weight.reshape(1024, 256),
        fine_act[0].reshape(24, 8, 64, 128),
    )
    factor = 1.0 / math.sqrt(lax.axis_size("dp") * lax.axis_size("dom") * slots * voxels)
    total = red.reshape(1024, 256).astype(F32) * factor
    return (fg.reshape(fine_act.shape), total[:864], total[864:992])


def solution(mesh):
    return jax.shard_map(
        body,
        mesh=mesh,
        in_specs=(
            P("dp", "dom", None, None),
            P("dp", "dom", None, None),
            P(),
            P(),
            P("dp", "dom", None, None),
            P("dp", "dom", None),
            P("dp", "dom", None, None),
        ),
        out_specs=(P("dp", "dom", None, None), P("dp", None), P("dp", None)),
        check_vma=False,
    )
```

time: 588 us -> 88 us (0.15); the launches traced: 579 us -> 87.9 us
  local copies, waits for them, and re-layouts: 214 us -> 5.82 us
  waiting for transfers between devices: 158 us -> 0 us
  matrix products: 102 us -> 0 us
  Pallas kernels: 0 us -> 80 us
  other arithmetic: 76.9 us -> 1.34 us
  between operations: 15 us -> 0.66 us
  starting transfers between devices: 12.3 us -> 0 us
    psum x1 -> x0, waiting for transfers between devices: 158 us -> none  [body(): conv_sum, down_sum = lax.psum((conv_part, down_part), ('dp', 'dom'))]
    dot_general x56 -> x0, matrix products: 102 us -> none  [the longest x27 76.9 us: correlate(): lax.dot_general(slabs[index_x], weight[position], (((1,), (1,)), ((), ())...]
    gather x89 -> x0, local copies, waits for them, and re-layouts: 98 us -> none  [pick_rows(): return extended[jnp.where(slot_index < 0, source.shape[0], slot_index)]]
    pallas_call x0 -> x1, Pallas kernels: none -> 80 us  [body(): pl.pallas_call(kernel, out_shape=(jax.ShapeDtypeStruct((24, 8, 64, 128),...]
    reshape x14 -> x0, local copies, waits for them, and re-layouts: 53.5 us -> none  [the longest x9 38.1 us: correlate(): plane_sum.reshape(count_blocks, block_edge, span, span, weight.shape[1])]
    concatenate x8 -> x0, other arithmetic: 32.2 us -> none  [the longest x4 21.7 us: assemble(): return jnp.concatenate(parts_x, axis=1)]
    unnamed x155 -> x5, local copies, waits for them, and re-layouts: 26.8 us -> 4.19 us
    gather x14 -> x0, other arithmetic: 16.2 us -> none  [pick_rows(): return extended[jnp.where(slot_index < 0, source.shape[0], slot_index)]]
  transfers between devices with their start and end apart: 5 -> 0, of which waited for: 1 -> 0; matrix products, arithmetic and copies ran while one was open for 28% -> 0% of each run, Pallas kernels for 0% -> 0%
where the time goes in v1:
time: 88 us; the launch traced here: 87.9 us
  Pallas kernels  80 us (91%)
  local copies, waits for them, and re-layouts  5.82 us (7%)
  other arithmetic  1.34 us (2%)
    pallas_call x1, Pallas kernels, body(): pl.pallas_call(kernel, out_shape=(jax.ShapeDtypeStruct((24, 8, 64, 128),...  80 us
    unnamed x5, local copies, waits for them, and re-layouts  4.19 us

profile of v1, /device:TPU:0, one launch (start us, length us, event | category | flops | bytes accessed | tf_op | source)
XLA Modules:
  0.0 87.9 jit_solution(5889919585312726263)
XLA Ops:
  0.6 1.3 %copy.15 = s32[1,3,27]{2,1,0:T(4,128)} copy(s32[1,3,27]{2,0,1:T(1,128)} %param.12) | data formatting | bytes 648
  1.9 1.3 %copy.14 = s32[1,1,3,8]{3,2,1,0:T(4,128)} copy(s32[1,1,3,8]{3,1,2,0:T(1,128)} %param.13) | data formatting | bytes 192
  3.1 80.0 %backward.1 = (bf16[24,8,64,128]{3,2,1,0:T(8,128)(2,1)}, bf16[4,4,4,16,256]{4,3,2,1,0:T(8,128)(2,1)}) custom-call(s32[3,27]{1,0:T(4,128)} %bitcast.19, s32[3,8]{1,0:T(4,128)} %bitcast.20, bf16[3,8,64,256]{3,2,1,0:T(8,128)(2,1)} %bitcast.16, bf16[3,8,64,256]{3,2,1,0:T(8,128)(2,1)} %bitcast.17, bf16[27,256,256]{2,1,0:T(8,128)(2,1)} %w_hbm.1, ...), custom_call_target="tpu_custom_call" | custom-call | tf_op jit(solution)/shard_map/backward/pallas_call | solution.py:397
  83.2 0.0 copy-start
  83.2 1.3 %convert_multiply_fusion = f32[4,4,4,16,256]{4,3,2,1,0:T(8,128)S(1)} fusion(bf16[4,4,4,16,256]{4,3,2,1,0:T(8,128)(2,1)} %get-tuple-element.6), kind=kLoop, calls=%fused_computation | loop fusion | flops 524288 | bytes 1572864 | tf_op jit(solution)/shard_map/mul | solution.py:453
  84.6 0.7 slice.9
  85.2 1.0 %slice.8 = f32[864,256]{1,0:T(8,128)} slice(f32[1024,256]{1,0:T(8,128)S(1)} %bitcast.13), slice={[0:864], [0:256]} | slice | bytes 1769472 | tf_op jit(solution)/shard_map/slice | solution.py:454
  86.2 0.0 copy-done
  86.2 1.7 %copy.17 = bf16[1,24,512,128]{3,2,1,0:T(8,128)(2,1)} copy(bf16[1,24,512,128]{3,2,1,0:T(8,128)(2,1)S(1)} %bitcast.14) | data formatting | bytes 6291456
Async XLA Ops:
  83.2 3.0 %copy-start = (bf16[24,8,64,128]{3,2,1,0:T(8,128)(2,1)S(1)}, bf16[24,8,64,128]{3,2,1,0:T(8,128)(2,1)}, u32[]{:S(2)}) copy-start(bf16[24,8,64,128]{3,2,1,0:T(8,128)(2,1)} %get-tuple-element.5) | copy-start | bytes 9437188

commit v2 on v1

v2 whole, which is shorter than its diff:
```python
import math

import jax
import jax.numpy as jnp
from jax import lax
from jax.experimental import pallas as pl
from jax.experimental.pallas import tpu as pltpu
from jax.sharding import PartitionSpec as P

MESH = pl.DeviceIdType.MESH
BF = jnp.bfloat16
F32 = jnp.float32
CAP = 3
GROUPS = 4
FIRST = "xyzz"


def dot_nt(a, b):
    return lax.dot_general(a, b, (((1,), (1,)), ((), ())), preferred_element_type=F32)


def dot_nn(a, b):
    return lax.dot_general(a, b, (((1,), (0,)), ((), ())), preferred_element_type=F32)


def kernel(
    links, routes, g_hbm, p_hbm, w_hbm, dw_hbm, fine_hbm,
    fg_hbm, conv_hbm, down_hbm,
    g, p, face, pface, gsh, ash, gt, w, dw, fine, fg, acc, octs, out, octin, ot,
    part, rcore, racc, r1, s1, a1, r2, red, conv,
    load_sem, halo_s, halo_r, oct_s, oct_r, red_s, red_r, fg_sem,
):
    dp = lax.axis_index("dp")
    dom = lax.axis_index("dom")
    zc, cc = dp // 2, dp % 2
    yc, xc = dom // 4, dom % 4
    coord = {"z": zc, "x": xc, "y": yc}

    def at_offset(**offsets):
        z, x, y = (lax.rem(coord[a] + offsets.get(a, 0), 4) for a in "zxy")
        return (z * 2 + cc, y * 4 + x)

    partner = (zc * 2 + (1 - cc), dom)
    nxt = (dp, lax.rem(dom + 1, 16))
    prv = (dp, lax.rem(dom + 15, 16))

    barrier = pltpu.get_barrier_semaphore()
    peers = [partner, nxt, prv]
    for z in range(4):
        for x in range(4):
            for y in range(4):
                if (z, x, y) != (0, 0, 0) and 0 in (z, x, y):
                    peers.append(at_offset(z=z, x=x, y=y))
    for peer in peers:
        pl.semaphore_signal(barrier, inc=1, device_id=peer, device_id_type=MESH)

    loads = []
    for i, (src, dst) in enumerate(
        ((g_hbm, g.at[0:CAP]), (p_hbm, p.at[0:CAP]), (w_hbm, w), (fine_hbm, fine), (dw_hbm, dw))
    ):
        c = pltpu.make_async_copy(src, dst, load_sem.at[i])
        c.start()
        loads.append(c)
    g[CAP] = jnp.zeros(g.shape[1:], BF)
    p[CAP] = jnp.zeros(p.shape[1:], BF)
    for i in range(2):
        face[i, CAP] = jnp.zeros(face.shape[2:], BF)
        pface[i, CAP] = jnp.zeros(face.shape[2:], BF)
    octs[24] = jnp.zeros(octs.shape[1:], BF)
    for s in range(8):
        part[3, s // 2, s % 2, 3, 2:4] = jnp.zeros((2, 16, 256), BF)
    loads[0].wait()
    loads[1].wait()
    pl.semaphore_wait(barrier, len(peers))

    def rcopy(src, dst, ss, rs, to):
        return pltpu.make_async_remote_copy(
            src_ref=src, dst_ref=dst, send_sem=ss, recv_sem=rs, device_id=to, device_id_type=MESH
        )

    halos = []
    for i, (src, dst, to) in enumerate(
        (
            (g.at[0:CAP, 7], face.at[0], nxt),
            (g.at[0:CAP, 0], face.at[1], prv),
            (p.at[0:CAP, 7], pface.at[0], nxt),
            (p.at[0:CAP, 0], pface.at[1], prv),
        )
    ):
        c = rcopy(src, dst.at[0:CAP], halo_s.at[i], halo_r.at[i], to)
        c.start()
        halos.append(c)

    zi = lax.broadcasted_iota(jnp.int32, (10, 8, 256), 1)

    def expand(load, a, blk, plane, dst, relu):
        def slot(b, c):
            n = links[blk, 0, 9 * (a + 1) + 3 * (b + 1) + (c + 1)]
            return jnp.where(n < 0, CAP, n)

        cols = []
        for c in (-1, 0, 1):
            low = load(slot(-1, c), pl.ds(48, 16)).astype(F32)[8:16]
            mid = load(slot(0, c), pl.ds(0, 64)).astype(F32)
            high = load(slot(1, c), pl.ds(0, 16)).astype(F32)[0:8]
            col = jnp.concatenate([low, mid, high], axis=0)
            if relu:
                col = jnp.maximum(col, 0.0)
            cols.append(col.reshape(10, 8, 256))
        shifted = (
            pltpu.roll(jnp.where(zi == 7, cols[0], cols[1]), 1, 1),
            cols[1],
            pltpu.roll(jnp.where(zi == 0, cols[2], cols[1]), 7, 1),
        )
        rows = pl.ds(pl.multiple_of(blk * 64, 64), 64)
        for ty in range(3):
            for tz in range(3):
                dst[3 * ty + tz, plane, rows] = shifted[tz][ty : ty + 8].reshape(64, 256).astype(BF)

    def inner_g(n, _):
        blk, x = n // 8, n % 8
        expand(lambda s, r: g[s, x, r], 0, blk, x + 1, gsh, False)
        return 0

    def outer_g(blk, _):
        expand(lambda s, r: face[0, s, r], -1, blk, 0, gsh, False)
        expand(lambda s, r: face[1, s, r], 1, blk, 9, gsh, False)
        return 0

    def inner_p(n, _):
        blk, x = n // 8, n % 8
        expand(lambda s, r: p[s, x, r], 0, blk, x + 1, ash, True)
        return 0

    def outer_p(blk, _):
        expand(lambda s, r: pface[0, s, r], -1, blk, 0, ash, True)
        expand(lambda s, r: pface[1, s, r], 1, blk, 9, ash, True)
        return 0

    def input_grad(half, first, last):
        def taps(n, _):
            tx, ty = n // 3, n % 3
            lhs = jnp.concatenate(
                [
                    gsh[8 - 3 * ty - tz, pl.ds(2 - tx + 4 * half, 4)].reshape(768, 256)
                    for tz in range(3)
                ],
                axis=1,
            )
            rhs = jnp.concatenate([w[3 * n + tz] for tz in range(3)], axis=1)
            acc[half] += dot_nt(lhs, rhs)
            return 0

        lax.fori_loop(first, last, taps, 0)

    lower = lax.broadcasted_iota(jnp.int32, (2, 8, 256), 1) < 4

    def octants(half):
        def plane(n, _):
            cx, blk = n // CAP, n % CAP
            val = acc[half, pl.ds(pl.multiple_of(n * 64, 64), 64)]
            pre = p[blk, 4 * half + cx].astype(F32)
            val = jnp.where(pre > 0.0, val, 0.0).reshape(2, 2, 2, 8, 256)
            for oy in range(2):
                even, odd = val[oy, :, 0], val[oy, :, 1]
                first = jnp.where(lower, even, pltpu.roll(odd, 4, 1))
                second = jnp.where(lower, pltpu.roll(even, 4, 1), odd)
                rows = pl.ds(pl.multiple_of(cx * 16, 16), 16)
                slot = blk * 8 + 4 * half + 2 * oy
                octs[slot, rows] = first.reshape(16, 256).astype(BF)
                octs[slot + 1, rows] = second.reshape(16, 256).astype(BF)
            return 0

        lax.fori_loop(0, 4 * CAP, plane, 0)

    passing = []

    def route(half):
        def place(k):
            def one(j, _):
                e = routes[0, k, 0, j]
                val = octs[jnp.where(e < 0, 24, e)]
                if k == 1:
                    octin[8 + j] = val
                else:
                    out[k // 2, j] = val
                return 0

            lax.fori_loop(4 * half, 4 * half + 4, one, 0)

        place(0)
        place(2)
        for k, base, to in ((0, 0, prv), (1, 16, nxt)):
            i = 2 * half + k
            c = rcopy(
                out.at[k, 4 * half : 4 * half + 4],
                octin.at[base + 4 * half : base + 4 * half + 4],
                oct_s.at[i], oct_r.at[i], to,
            )
            c.start()
            passing.append(c)
        place(1)

    acc[...] = jnp.zeros(acc.shape, F32)
    lax.fori_loop(0, CAP * 8, inner_g, 0)
    loads[2].wait()
    input_grad(0, 3, 6)
    input_grad(1, 3, 6)
    halos[0].wait_recv()
    halos[1].wait_recv()
    lax.fori_loop(0, CAP, outer_g, 0)
    for half in range(2):
        input_grad(half, 0, 3)
        input_grad(half, 6, 9)
        octants(half)
        route(half)

    lax.fori_loop(0, CAP * 8, inner_p, 0)
    halos[2].wait_recv()
    halos[3].wait_recv()
    lax.fori_loop(0, CAP, outer_p, 0)

    def transpose_plane(x, _):
        gt[:, pl.ds(pl.multiple_of(x * 384, 384), 384)] = (
            gsh[4, pl.ds(1 + 2 * x, 2)].reshape(384, 256).T
        )
        return 0

    lax.fori_loop(0, 4, transpose_plane, 0)

    def tap(t):
        tx, tyz = t // 9, t % 9
        rows = ash[tyz, pl.ds(tx, 8)].reshape(1536, 256)
        return dot_nn(gt[...], rows).T.astype(BF)

    def whole_tap(shift):
        def one(k, _):
            part[shift, k // 2, k % 2] = tap((27 * k + 7) // 8 + shift).reshape(4, 4, 16, 256)
            return 0

        return one

    def split_tap(n, _):
        t = 2 + n
        for at, jump in ((2, 2), (3, 2), (5, 2), (6, 2), (7, 2), (9, 2), (10, 2)):
            t = t + jnp.where(n >= at, jump, 0)
        grad = tap(t)
        for i in range(8):
            m = t * 8 + i
            k, r = m // 27, m % 27
            pos = jnp.where(t < (27 * k + 7) // 8, r, r - 16)
            q8 = pos % 8
            part[2 + pos // 8, k // 2, k % 2, q8 // 2, pl.ds((q8 % 2) * 2, 2)] = grad[
                32 * i : 32 * i + 32
            ].reshape(2, 16, 256)
        return 0

    def cut(ref, axis, at):
        return ref.at[tuple(at if d == axis else slice(None) for d in "zxy")]

    class Group:
        def __init__(self, grp):
            self.grp = grp
            self.axis = FIRST[grp]
            self.stage = 0
            self.sends = []

        def send(self, src, dst, i, to):
            c = rcopy(src, dst, red_s.at[self.grp, i], red_r.at[self.grp, i], to)
            c.start()
            if i < 7:
                self.sends.append(c)
            return c

        def all_of(self, i):
            return rcopy(
                r2.at[self.grp], r2.at[self.grp], red_s.at[self.grp, i], red_r.at[self.grp, i],
                partner,
            )

        def chunk(self, off, half):
            ref = cut(racc.at[self.grp], self.axis, lax.rem(coord[self.axis] + off, 4))
            return ref.at[2 * half : 2 * half + 2]

        def step(self):
            grp, axis = self.grp, self.axis
            left, right = at_offset(**{axis: 3}), at_offset(**{axis: 1})
            stage = self.stage
            self.stage += 1
            if stage == 0:
                self.core = self.send(part.at[grp, :, 1 - cc], rcore.at[grp], 0, partner)
            elif stage == 1:
                self.core.wait_recv()
                for z in range(4):
                    racc[grp, z] = (
                        part[grp, z, cc].astype(F32) + rcore[grp, z].astype(F32)
                    ).astype(BF)
                box = r1.at[grp]
                self.relay_a = self.send(self.chunk(2, 0), box.at[0], 1, right)
                self.relay_b = self.send(self.chunk(2, 1), box.at[1], 2, left)
                self.direct_b = self.send(self.chunk(1, 1), box.at[2], 3, right)
                self.direct_a = self.send(self.chunk(3, 0), box.at[3], 4, left)
            elif stage == 2:
                box = r1.at[grp]
                self.relay_a.wait_recv()
                s1[grp, 0] = (self.chunk(1, 0)[...].astype(F32) + r1[grp, 0].astype(F32)).astype(BF)
                self.sum_a = self.send(s1.at[grp, 0], box.at[4], 5, right)
                self.relay_b.wait_recv()
                s1[grp, 1] = (self.chunk(3, 1)[...].astype(F32) + r1[grp, 1].astype(F32)).astype(BF)
                self.sum_b = self.send(s1.at[grp, 1], box.at[5], 6, left)
            elif stage == 3:
                for c in (self.direct_a, self.direct_b, self.sum_a, self.sum_b):
                    c.wait_recv()
                for half, (i, j) in enumerate(((4, 3), (5, 2))):
                    total = self.chunk(0, half)[...].astype(F32)
                    total = total + r1[grp, i].astype(F32) + r1[grp, j].astype(F32)
                    a1[grp, 2 * half : 2 * half + 2] = total.astype(BF)
                u, v = "zxy".replace(axis, "")
                for n in range(1, 16):
                    du, dv = n // 4, n % 4
                    src = a1.at[grp, lax.rem(coord[u] + du, 4), lax.rem(coord[v] + dv, 4)]
                    self.send(src, r2.at[grp, n - 1], 7, at_offset(**{u: du, v: dv}))
            elif stage == 4:
                self.all_of(7).wait_recv()
                u, v = "zxy".replace(axis, "")
                total = a1[grp, coord[u], coord[v]].astype(F32)
                for n in range(15):
                    total = total + r2[grp, n].astype(F32)
                red[grp, xc, yc] = total.astype(BF)
                spot = red.at[grp, xc, yc]
                for n in range(1, 16):
                    self.send(spot, spot, 8, at_offset(x=n // 4, y=n % 4))
            else:
                self.all_of(8).wait_recv()

        def finish(self):
            for c in self.sends:
                c.wait_send()
            self.all_of(7).wait_send()
            self.all_of(8).wait_send()

    ga, gb, gc, gd = (Group(i) for i in range(GROUPS))

    lax.fori_loop(0, 11, split_tap, 0)
    gc.step()
    lax.fori_loop(0, 8, whole_tap(0), 0)
    ga.step()
    gc.step()
    lax.fori_loop(0, 4, whole_tap(1), 0)
    gc.step()
    ga.step()
    lax.fori_loop(4, 8, whole_tap(1), 0)
    gb.step()

    for c in passing:
        c.wait_recv()
    loads[3].wait()
    loads[4].wait()

    def turn(i, _):
        ot[:, pl.ds(pl.multiple_of(i * 384, 384), 384)] = (
            octin[pl.ds(6 * i, 6)].reshape(384, 256).T
        )
        return 0

    lax.fori_loop(0, 4, turn, 0)

    def down(i, _):
        rows = jnp.concatenate(
            [fine[:, 2 * i].reshape(1536, 128), fine[:, 2 * i + 1].reshape(1536, 128)], axis=1
        )
        grad = dot_nn(ot[...], rows).T.astype(BF)
        for c in range(2):
            one = grad[128 * c : 128 * c + 128]
            part[3, i, c, 1, 2:4] = one[0:32].reshape(2, 16, 256)
            part[3, i, c, 2] = one[32:96].reshape(4, 16, 256)
            part[3, i, c, 3, 0:2] = one[96:128].reshape(2, 16, 256)
        return 0

    lax.fori_loop(0, 4, down, 0)
    gd.step()
    gc.step()
    ga.step()

    def fine_grad(i, _):
        at = pl.ds(4 * i, 4)
        res = dot_nt(octin[at].reshape(256, 256), dw[...]).astype(BF)
        for q in range(8):
            fg[at, q] = res[:, 128 * q : 128 * q + 128].reshape(4, 64, 128)
        return 0

    puts = []

    def fine_part(i):
        lax.fori_loop(2 * i, 2 * i + 2, fine_grad, 0)
        c = pltpu.make_async_copy(
            fg.at[8 * i : 8 * i + 8], fg_hbm.at[8 * i : 8 * i + 8], fg_sem.at[i]
        )
        c.start()
        puts.append(c)

    fine_part(0)
    gb.step()
    fine_part(1)
    gd.step()
    fine_part(2)
    for one in (ga, gc, gb, gd, gb, ga, gd, gc, gb, ga, gd, gb, gd):
        one.step()

    k = dp
    lead = (27 * k + 7) // 8 * 8 - 27 * k
    start = pl.multiple_of(lead * 32, 32)
    conv[pl.ds(start, 256)] = red[0].reshape(256, 256)
    conv[pl.ds(start + 256, 256)] = red[1].reshape(256, 256)
    for n in range(11):
        row = 32 * (n + jnp.where(n < lead, 0, 16))
        piece = red[2 + n // 8, n % 8 // 2, (n % 2) * 2 : (n % 2) * 2 + 2]
        conv[pl.ds(pl.multiple_of(row, 32), 32)] = piece.reshape(32, 256)
    conv[864:896] = red[3, 1, 2:4].reshape(32, 256)
    conv[896:960] = red[3, 2].reshape(64, 256)
    conv[960:992] = red[3, 3, 0:2].reshape(32, 256)
    for i, (src, dst) in enumerate(((conv.at[0:864], conv_hbm), (conv.at[864:992], down_hbm))):
        c = pltpu.make_async_copy(src, dst, fg_sem.at[3 + i])
        c.start()
        puts.append(c)
    for c in halos + passing:
        c.wait_send()
    for one in (ga, gb, gc, gd):
        one.finish()
    for c in puts:
        c.wait()


def body(grad_out, pre_act, conv_weight, down_weight, fine_act, neighbours, octant_routes):
    slots, voxels, channels = grad_out.shape[1:]
    any_space = pl.BlockSpec(memory_space=pl.ANY)
    smem = pl.BlockSpec(memory_space=pltpu.SMEM)
    V = pltpu.VMEM
    fg, conv, down = pl.pallas_call(
        kernel,
        out_shape=(
            jax.ShapeDtypeStruct((24, 8, 64, 128), BF),
            jax.ShapeDtypeStruct((864, 256), BF),
            jax.ShapeDtypeStruct((128, 256), BF),
        ),
        in_specs=[smem, smem] + [any_space] * 5,
        out_specs=(any_space, any_space, any_space),
        scratch_shapes=[
            V((CAP + 1, 8, 64, 256), BF),
            V((CAP + 1, 8, 64, 256), BF),
            V((2, CAP + 1, 64, 256), BF),
            V((2, CAP + 1, 64, 256), BF),
            V((9, 10, 192, 256), BF),
            V((9, 10, 192, 256), BF),
            V((256, 1536), BF),
            V((27, 256, 256), BF),
            V((1024, 256), BF),
            V((24, 8, 64, 128), BF),
            V((24, 8, 64, 128), BF),
            V((2, 768, 256), F32),
            V((25, 64, 256), BF),
            V((2, 8, 64, 256), BF),
            V((24, 64, 256), BF),
            V((256, 1536), BF),
            V((GROUPS, 4, 2, 4, 4, 16, 256), BF),
            V((GROUPS, 4, 4, 4, 16, 256), BF),
            V((GROUPS, 4, 4, 4, 16, 256), BF),
            V((GROUPS, 6, 2, 4, 16, 256), BF),
            V((GROUPS, 2, 2, 4, 16, 256), BF),
            V((GROUPS, 4, 4, 16, 256), BF),
            V((GROUPS, 15, 16, 256), BF),
            V((GROUPS, 4, 4, 16, 256), BF),
            V((992, 256), BF),
            pltpu.SemaphoreType.DMA((5,)),
            pltpu.SemaphoreType.DMA((4,)),
            pltpu.SemaphoreType.DMA((4,)),
            pltpu.SemaphoreType.DMA((4,)),
            pltpu.SemaphoreType.DMA((4,)),
            pltpu.SemaphoreType.DMA((GROUPS, 9)),
            pltpu.SemaphoreType.DMA((GROUPS, 9)),
            pltpu.SemaphoreType.DMA((5,)),
        ],
        compiler_params=pltpu.CompilerParams(
            collective_id=0, has_side_effects=True, vmem_limit_bytes=60 * 1024 * 1024
        ),
        name="backward",
    )(
        neighbours.transpose(1, 0, 2),
        octant_routes.transpose(0, 2, 1, 3),
        grad_out[0].reshape(slots, 8, 64, channels),
        pre_act[0].reshape(slots, 8, 64, channels),
        conv_weight,
        down_weight.reshape(1024, 256),
        fine_act[0].reshape(24, 8, 64, 128),
    )
    factor = 1.0 / math.sqrt(lax.axis_size("dp") * lax.axis_size("dom") * slots * voxels)
    return (fg.reshape(fine_act.shape), conv.astype(F32) * factor, down.astype(F32) * factor)


def solution(mesh):
    return jax.shard_map(
        body,
        mesh=mesh,
        in_specs=(
            P("dp", "dom", None, None),
            P("dp", "dom", None, None),
            P(),
            P(),
            P("dp", "dom", None, None),
            P("dp", "dom", None),
            P("dp", "dom", None, None),
        ),
        out_specs=(P("dp", "dom", None, None), P("dp", None), P("dp", None)),
        check_vma=False,
    )
```

time: 88 us -> 75.4 us (0.86)
  Pallas kernels: 80 us -> 67.1 us
  other arithmetic: 1.34 us -> 3.51 us
  local copies, waits for them, and re-layouts: 5.82 us -> 3.86 us
    pallas_call x1, Pallas kernels: 80 us -> 67.1 us  [body(): pl.pallas_call(kernel, out_shape=(jax.ShapeDtypeStruct((24, 8, 64, 128),...]
    mul x1 -> x2, other arithmetic: 1.34 us -> 3.51 us  [the longest x1 2 us: body(): conv.astype(F32) * factor]
    slice x2 -> x0, local copies, waits for them, and re-layouts: 1.64 us -> none  [body(): return (fg.reshape(fine_act.shape), total[:864], total[864:992])]
    unnamed x5 -> x1, local copies, waits for them, and re-layouts: 4.19 us -> 3.86 us
where the time goes in v2:
time: 75.4 us; the launch traced here: 75.1 us
  Pallas kernels  67.1 us (89%)
  local copies, waits for them, and re-layouts  3.86 us (5%)
  other arithmetic  3.51 us (5%)
    pallas_call x1, Pallas kernels, body(): pl.pallas_call(kernel, out_shape=(jax.ShapeDtypeStruct((24, 8, 64, 128),...  67.1 us
    unnamed x1, local copies, waits for them, and re-layouts  3.86 us
    mul x1, other arithmetic, body(): conv.astype(F32) * factor  2 us

profile of v2, /device:TPU:0, one launch (start us, length us, event | category | flops | bytes accessed | tf_op | source)
XLA Modules:
  0.0 75.1 jit_solution(12188676406454326338)
XLA Ops:
  0.6 67.1 %backward.1 = (bf16[24,8,64,128]{3,2,1,0:T(8,128)(2,1)}, bf16[864,256]{1,0:T(8,128)(2,1)}, bf16[128,256]{1,0:T(8,128)(2,1)}) custom-call(s32[3,1,27]{2,1,0:T(1,128)} %bitcast.12, s32[1,3,1,8]{3,2,1,0:T(1,128)} %bitcast.13, bf16[3,8,64,256]{3,2,1,0:T(8,128)(2,1)} %bitcast.9, bf16[3,8,64,256]{3,2,1,0:T(8,128)(2,1)} %bitcast.10, bf16[27,256,256]{2,1,0:T(8,128)(2,1)} %w_hbm.1, ...), custom_call_target="tpu_custom_call" | custom-call | tf_op jit(solution)/shard_map/backward/pallas_call | solution.py:439
  67.8 1.5 %convert_multiply_fusion.1 = f32[128,256]{1,0:T(8,128)} fusion(bf16[128,256]{1,0:T(8,128)(2,1)} %get-tuple-element.8), kind=kLoop, calls=%fused_computation.1 | loop fusion | flops 65536 | bytes 196608 | tf_op jit(solution)/shard_map/mul | solution.py:497
  69.3 2.0 %convert_multiply_fusion = f32[864,256]{1,0:T(8,128)} fusion(bf16[864,256]{1,0:T(8,128)(2,1)} %get-tuple-element.7), kind=kLoop, calls=%fused_computation | loop fusion | flops 442368 | bytes 1327104 | tf_op jit(solution)/shard_map/mul | solution.py:497
  71.3 3.9 %copy.11 = bf16[1,24,512,128]{3,2,1,0:T(8,128)(2,1)} copy(bf16[1,24,512,128]{3,2,1,0:T(8,128)(2,1)} %bitcast.8) | data formatting | bytes 6291456

commit v3 on v2

--- a/solution.py
+++ b/solution.py
@@ -12,7 +12,7 @@
 F32 = jnp.float32
 CAP = 3
 GROUPS = 4
-FIRST = "xyzz"
+FLOWS = ((2, 0, 256, "z"), (3, 0, 128, "y"), (3, 128, 128, "x"), (0, 0, 256, "x"), (1, 0, 128, "z"), (1, 128, 128, "y"))
 
 
 def dot_nt(a, b):
@@ -24,11 +24,11 @@
 
 
 def kernel(
-    links, routes, g_hbm, p_hbm, w_hbm, dw_hbm, fine_hbm,
-    fg_hbm, conv_hbm, down_hbm,
-    g, p, face, pface, gsh, ash, gt, w, dw, fine, fg, acc, octs, out, octin, ot,
+    links, routes, g_hbm, p_hbm, w_hbm, fine_hbm,
+    octin_hbm, conv_hbm, down_hbm,
+    g, p, face, pface, gsh, ash, gt, w, fine, acc, octs, out, octin, ot,
     part, rcore, racc, r1, s1, a1, r2, red, conv,
-    load_sem, halo_s, halo_r, oct_s, oct_r, red_s, red_r, fg_sem,
+    load_sem, halo_s, halo_r, oct_s, oct_r, red_s, red_r, put_sem,
 ):
     dp = lax.axis_index("dp")
     dom = lax.axis_index("dom")
@@ -56,7 +56,7 @@
 
     loads = []
     for i, (src, dst) in enumerate(
-        ((g_hbm, g.at[0:CAP]), (p_hbm, p.at[0:CAP]), (w_hbm, w), (fine_hbm, fine), (dw_hbm, dw))
+        ((g_hbm, g.at[0:CAP]), (p_hbm, p.at[0:CAP]), (w_hbm, w), (fine_hbm, fine))
     ):
         c = pltpu.make_async_copy(src, dst, load_sem.at[i])
         c.start()
@@ -71,25 +71,11 @@
         part[3, s // 2, s % 2, 3, 2:4] = jnp.zeros((2, 16, 256), BF)
     loads[0].wait()
     loads[1].wait()
-    pl.semaphore_wait(barrier, len(peers))
 
     def rcopy(src, dst, ss, rs, to):
         return pltpu.make_async_remote_copy(
             src_ref=src, dst_ref=dst, send_sem=ss, recv_sem=rs, device_id=to, device_id_type=MESH
         )
-
-    halos = []
-    for i, (src, dst, to) in enumerate(
-        (
-            (g.at[0:CAP, 7], face.at[0], nxt),
-            (g.at[0:CAP, 0], face.at[1], prv),
-            (p.at[0:CAP, 7], pface.at[0], nxt),
-            (p.at[0:CAP, 0], pface.at[1], prv),
-        )
-    ):
-        c = rcopy(src, dst.at[0:CAP], halo_s.at[i], halo_r.at[i], to)
-        c.start()
-        halos.append(c)
 
     zi = lax.broadcasted_iota(jnp.int32, (10, 8, 256), 1)
 
@@ -203,6 +189,21 @@
 
     acc[...] = jnp.zeros(acc.shape, F32)
     lax.fori_loop(0, CAP * 8, inner_g, 0)
+    pl.semaphore_wait(barrier, len(peers))
+
+    halos = []
+    for i, (src, dst, to) in enumerate(
+        (
+            (g.at[0:CAP, 7], face.at[0], nxt),
+            (g.at[0:CAP, 0], face.at[1], prv),
+            (p.at[0:CAP, 7], pface.at[0], nxt),
+            (p.at[0:CAP, 0], pface.at[1], prv),
+        )
+    ):
+        c = rcopy(src, dst.at[0:CAP], halo_s.at[i], halo_r.at[i], to)
+        c.start()
+        halos.append(c)
+
     loads[2].wait()
     input_grad(0, 3, 6)
     input_grad(1, 3, 6)
@@ -258,76 +259,81 @@
     def cut(ref, axis, at):
         return ref.at[tuple(at if d == axis else slice(None) for d in "zxy")]
 
-    class Group:
-        def __init__(self, grp):
-            self.grp = grp
-            self.axis = FIRST[grp]
+    class Flow:
+        def __init__(self, n):
+            self.n = n
+            grp, lane, width, self.axis = FLOWS[n]
+            lanes = pl.ds(lane, width)
+            self.part = part.at[grp, :, :, :, :, :, lanes]
+            self.rcore = rcore.at[grp, :, :, :, :, lanes]
+            self.racc = racc.at[grp, :, :, :, :, lanes]
+            self.r1 = r1.at[grp, :, :, :, :, lanes]
+            self.s1 = s1.at[grp, :, :, :, :, lanes]
+            self.a1 = a1.at[grp, :, :, :, lanes]
+            self.r2 = r2.at[grp, :, :, lanes]
+            self.red = red.at[grp, :, :, :, lanes]
             self.stage = 0
             self.sends = []
 
         def send(self, src, dst, i, to):
-            c = rcopy(src, dst, red_s.at[self.grp, i], red_r.at[self.grp, i], to)
+            c = rcopy(src, dst, red_s.at[self.n, i], red_r.at[self.n, i], to)
             c.start()
             if i < 7:
                 self.sends.append(c)
             return c
 
         def all_of(self, i):
-            return rcopy(
-                r2.at[self.grp], r2.at[self.grp], red_s.at[self.grp, i], red_r.at[self.grp, i],
-                partner,
-            )
+            return rcopy(self.r2, self.r2, red_s.at[self.n, i], red_r.at[self.n, i], partner)
 
         def chunk(self, off, half):
-            ref = cut(racc.at[self.grp], self.axis, lax.rem(coord[self.axis] + off, 4))
+            ref = cut(self.racc, self.axis, lax.rem(coord[self.axis] + off, 4))
             return ref.at[2 * half : 2 * half + 2]
 
         def step(self):
-            grp, axis = self.grp, self.axis
+            axis = self.axis
             left, right = at_offset(**{axis: 3}), at_offset(**{axis: 1})
+            u, v = "zxy".replace(axis, "")
             stage = self.stage
             self.stage += 1
             if stage == 0:
-                self.core = self.send(part.at[grp, :, 1 - cc], rcore.at[grp], 0, partner)
+                self.core = self.send(self.part.at[:, 1 - cc], self.rcore, 0, partner)
             elif stage == 1:
                 self.core.wait_recv()
                 for z in range(4):
-                    racc[grp, z] = (
-                        part[grp, z, cc].astype(F32) + rcore[grp, z].astype(F32)
+                    self.racc[z] = (
+                        self.part[z, cc].astype(F32) + self.rcore[z].astype(F32)
                     ).astype(BF)
-                box = r1.at[grp]
+                box = self.r1
                 self.relay_a = self.send(self.chunk(2, 0), box.at[0], 1, right)
                 self.relay_b = self.send(self.chunk(2, 1), box.at[1], 2, left)
                 self.direct_b = self.send(self.chunk(1, 1), box.at[2], 3, right)
                 self.direct_a = self.send(self.chunk(3, 0), box.at[3], 4, left)
             elif stage == 2:
-                box = r1.at[grp]
+                box = self.r1
                 self.relay_a.wait_recv()
-                s1[grp, 0] = (self.chunk(1, 0)[...].astype(F32) + r1[grp, 0].astype(F32)).astype(BF)
-                self.sum_a = self.send(s1.at[grp, 0], box.at[4], 5, right)
+                self.s1[0] = (self.chunk(1, 0)[...].astype(F32) + box[0].astype(F32)).astype(BF)
+                self.sum_a = self.send(self.s1.at[0], box.at[4], 5, right)
                 self.relay_b.wait_recv()
-                s1[grp, 1] = (self.chunk(3, 1)[...].astype(F32) + r1[grp, 1].astype(F32)).astype(BF)
-                self.sum_b = self.send(s1.at[grp, 1], box.at[5], 6, left)
+                self.s1[1] = (self.chunk(3, 1)[...].astype(F32) + box[1].astype(F32)).astype(BF)
+                self.sum_b = self.send(self.s1.at[1], box.at[5], 6, left)
             elif stage == 3:
                 for c in (self.direct_a, self.direct_b, self.sum_a, self.sum_b):
                     c.wait_recv()
                 for half, (i, j) in enumerate(((4, 3), (5, 2))):
                     total = self.chunk(0, half)[...].astype(F32)
-                    total = total + r1[grp, i].astype(F32) + r1[grp, j].astype(F32)
-                    a1[grp, 2 * half : 2 * half + 2] = total.astype(BF)
-                u, v = "zxy".replace(axis, "")
+                    total = total + self.r1[i].astype(F32) + self.r1[j].astype(F32)
+                    self.a1[2 * half : 2 * half + 2] = total.astype(BF)
                 for n in range(1, 16):
                     du, dv = n // 4, n % 4
-                    src = a1.at[grp, lax.rem(coord[u] + du, 4), lax.rem(coord[v] + dv, 4)]
-                    self.send(src, r2.at[grp, n - 1], 7, at_offset(**{u: du, v: dv}))
+                    src = self.a1.at[lax.rem(coord[u] + du, 4), lax.rem(coord[v] + dv, 4)]
+                    self.send(src, self.r2.at[n - 1], 7, at_offset(**{u: du, v: dv}))
             elif stage == 4:
                 self.all_of(7).wait_recv()
-                u, v = "zxy".replace(axis, "")
-                total = a1[grp, coord[u], coord[v]].astype(F32)
+                total = self.a1[coord[u], coord[v]].astype(F32)
                 for n in range(15):
-                    total = total + r2[grp, n].astype(F32)
-                red[grp, xc, yc] = total.astype(BF)
-                spot = red.at[grp, xc, yc]
+                    total = total + self.r2[n].astype(F32)
+                self.red[xc, yc] = total.astype(BF)
+                spot = self.red.at[xc, yc]
                 for n in range(1, 16):
                     self.send(spot, spot, 8, at_offset(x=n // 4, y=n % 4))
             else:
@@ -339,23 +345,28 @@
             self.all_of(7).wait_send()
             self.all_of(8).wait_send()
 
-    ga, gb, gc, gd = (Group(i) for i in range(GROUPS))
+    flows = [Flow(i) for i in range(len(FLOWS))]
+    fc, fa = flows[0:1], flows[3:4]
+    fd, fb = flows[1:3], flows[4:6]
+
+    def step(*some):
+        for group in some:
+            for one in group:
+                one.step()
 
     lax.fori_loop(0, 11, split_tap, 0)
-    gc.step()
-    lax.fori_loop(0, 8, whole_tap(0), 0)
-    ga.step()
-    gc.step()
-    lax.fori_loop(0, 4, whole_tap(1), 0)
-    gc.step()
-    ga.step()
-    lax.fori_loop(4, 8, whole_tap(1), 0)
-    gb.step()
-
+    step(fc)
     for c in passing:
         c.wait_recv()
+    puts = []
+
+    def put(src, dst):
+        c = pltpu.make_async_copy(src, dst, put_sem.at[len(puts)])
+        c.start()
+        puts.append(c)
+
+    put(octin, octin_hbm)
     loads[3].wait()
-    loads[4].wait()
 
     def turn(i, _):
         ot[:, pl.ds(pl.multiple_of(i * 384, 384), 384)] = (
@@ -378,34 +389,15 @@
         return 0
 
     lax.fori_loop(0, 4, down, 0)
-    gd.step()
-    gc.step()
-    ga.step()
-
-    def fine_grad(i, _):
-        at = pl.ds(4 * i, 4)
-        res = dot_nt(octin[at].reshape(256, 256), dw[...]).astype(BF)
-        for q in range(8):
-            fg[at, q] = res[:, 128 * q : 128 * q + 128].reshape(4, 64, 128)
-        return 0
-
-    puts = []
-
-    def fine_part(i):
-        lax.fori_loop(2 * i, 2 * i + 2, fine_grad, 0)
-        c = pltpu.make_async_copy(
-            fg.at[8 * i : 8 * i + 8], fg_hbm.at[8 * i : 8 * i + 8], fg_sem.at[i]
-        )
-        c.start()
-        puts.append(c)
-
-    fine_part(0)
-    gb.step()
-    fine_part(1)
-    gd.step()
-    fine_part(2)
-    for one in (ga, gc, gb, gd, gb, ga, gd, gc, gb, ga, gd, gb, gd):
-        one.step()
+    step(fd, fc)
+    lax.fori_loop(0, 4, whole_tap(0), 0)
+    step(fd)
+    lax.fori_loop(4, 8, whole_tap(0), 0)
+    step(fa, fc)
+    lax.fori_loop(0, 4, whole_tap(1), 0)
+    step(fa, fd, fc)
+    lax.fori_loop(4, 8, whole_tap(1), 0)
+    step(fb, fa, fd, fb, fc, fa, fd, fb, fc, fb, fa, fd, fb, fa, fb)
 
     k = dp
     lead = (27 * k + 7) // 8 * 8 - 27 * k
@@ -419,16 +411,22 @@
     conv[864:896] = red[3, 1, 2:4].reshape(32, 256)
     conv[896:960] = red[3, 2].reshape(64, 256)
     conv[960:992] = red[3, 3, 0:2].reshape(32, 256)
-    for i, (src, dst) in enumerate(((conv.at[0:864], conv_hbm), (conv.at[864:992], down_hbm))):
-        c = pltpu.make_async_copy(src, dst, fg_sem.at[3 + i])
-        c.start()
-        puts.append(c)
+    put(conv.at[0:864], conv_hbm)
+    put(conv.at[864:992], down_hbm)
     for c in halos + passing:
         c.wait_send()
-    for one in (ga, gb, gc, gd):
+    for one in flows:
         one.finish()
     for c in puts:
         c.wait()
+
+
+def final(scale, octin, dw, conv_in, down_in, fg, conv, down):
+    res = dot_nt(octin[...].reshape(256, 256), dw[...]).astype(BF)
+    for q in range(8):
+        fg[:, q] = res[:, 128 * q : 128 * q + 128].reshape(4, 64, 128)
+    conv[...] = conv_in[...].astype(F32) * scale
+    down[...] = down_in[...].astype(F32) * scale
 
 
 def body(grad_out, pre_act, conv_weight, down_weight, fine_act, neighbours, octant_routes):
@@ -436,14 +434,14 @@
     any_space = pl.BlockSpec(memory_space=pl.ANY)
     smem = pl.BlockSpec(memory_space=pltpu.SMEM)
     V = pltpu.VMEM
-    fg, conv, down = pl.pallas_call(
+    octin, conv, down = pl.pallas_call(
         kernel,
         out_shape=(
-            jax.ShapeDtypeStruct((24, 8, 64, 128), BF),
+            jax.ShapeDtypeStruct((24, 64, 256), BF),
             jax.ShapeDtypeStruct((864, 256), BF),
             jax.ShapeDtypeStruct((128, 256), BF),
         ),
-        in_specs=[smem, smem] + [any_space] * 5,
+        in_specs=[smem, smem] + [any_space] * 4,
         out_specs=(any_space, any_space, any_space),
         scratch_shapes=[
             V((CAP + 1, 8, 64, 256), BF),
@@ -454,8 +452,6 @@
             V((9, 10, 192, 256), BF),
             V((256, 1536), BF),
             V((27, 256, 256), BF),
-            V((1024, 256), BF),
-            V((24, 8, 64, 128), BF),
             V((24, 8, 64, 128), BF),
             V((2, 768, 256), F32),
             V((25, 64, 256), BF),
@@ -471,14 +467,14 @@
             V((GROUPS, 15, 16, 256), BF),
             V((GROUPS, 4, 4, 16, 256), BF),
             V((992, 256), BF),
-            pltpu.SemaphoreType.DMA((5,)),
             pltpu.SemaphoreType.DMA((4,)),
             pltpu.SemaphoreType.DMA((4,)),
             pltpu.SemaphoreType.DMA((4,)),
             pltpu.SemaphoreType.DMA((4,)),
-            pltpu.SemaphoreType.DMA((GROUPS, 9)),
-            pltpu.SemaphoreType.DMA((GROUPS, 9)),
-            pltpu.SemaphoreType.DMA((5,)),
+            pltpu.SemaphoreType.DMA((4,)),
+            pltpu.SemaphoreType.DMA((len(FLOWS), 9)),
+            pltpu.SemaphoreType.DMA((len(FLOWS), 9)),
+            pltpu.SemaphoreType.DMA((3,)),
         ],
         compiler_params=pltpu.CompilerParams(
             collective_id=0, has_side_effects=True, vmem_limit_bytes=60 * 1024 * 1024
@@ -490,11 +486,29 @@
         grad_out[0].reshape(slots, 8, 64, channels),
         pre_act[0].reshape(slots, 8, 64, channels),
         conv_weight,
-        down_weight.reshape(1024, 256),
         fine_act[0].reshape(24, 8, 64, 128),
     )
     factor = 1.0 / math.sqrt(lax.axis_size("dp") * lax.axis_size("dom") * slots * voxels)
-    return (fg.reshape(fine_act.shape), conv.astype(F32) * factor, down.astype(F32) * factor)
+    whole = pl.BlockSpec((128, 256), lambda i: (0, 0))
+    rows = pl.BlockSpec((144, 256), lambda i: (i, 0))
+    fg, conv, down = pl.pallas_call(
+        lambda *refs: final(factor, *refs),
+        out_shape=(
+            jax.ShapeDtypeStruct((24, 8, 64, 128), BF),
+            jax.ShapeDtypeStruct((864, 256), F32),
+            jax.ShapeDtypeStruct((128, 256), F32),
+        ),
+        grid=(6,),
+        in_specs=[
+            pl.BlockSpec((4, 64, 256), lambda i: (i, 0, 0)),
+            pl.BlockSpec((1024, 256), lambda i: (0, 0)),
+            rows,
+            whole,
+        ],
+        out_specs=(pl.BlockSpec((4, 8, 64, 128), lambda i: (i, 0, 0, 0)), rows, whole),
+        name="final",
+    )(octin, down_weight.reshape(1024, 256), conv, down)
+    return (fg.reshape(fine_act.shape), conv, down)
 
 
 def solution(mesh):

time: 75.4 us -> 73.9 us (0.980)
  Pallas kernels: 67.1 us -> 73 us
  local copies, waits for them, and re-layouts: 3.86 us -> 0 us
  other arithmetic: 3.51 us -> 0 us
    pallas_call x1 -> x2, Pallas kernels: 67.1 us -> 73 us  [the longest x1 67.1 us: body(): pl.pallas_call(kernel, out_shape=(jax.ShapeDtypeStruct((24, 64, 256), BF)...]
    unnamed x1 -> x0, local copies, waits for them, and re-layouts: 3.86 us -> none
    mul x2 -> x0, other arithmetic: 3.51 us -> none  [the longest x1 2 us: body(): conv.astype(F32) * factor]
where the time goes in v3:
time: 73.9 us; the launch traced here: 73.6 us
  Pallas kernels  73 us (99%)
    pallas_call x1, Pallas kernels, body(): pl.pallas_call(kernel, out_shape=(jax.ShapeDtypeStruct((24, 64, 256), BF)...  67.1 us
    pallas_call x1, Pallas kernels, body(): pl.pallas_call(lambda *refs: final(factor, *refs), out_shape=(jax.ShapeDt...  5.94 us

profile of v3, /device:TPU:0, one launch (start us, length us, event | category | flops | bytes accessed | tf_op | source)
XLA Modules:
  0.0 73.6 jit_solution(10027146139018646125)
XLA Ops:
  0.6 67.1 %backward.1 = (bf16[24,64,256]{2,1,0:T(8,128)(2,1)}, bf16[864,256]{1,0:T(8,128)(2,1)}, bf16[128,256]{1,0:T(8,128)(2,1)}) custom-call(s32[3,1,27]{2,1,0:T(1,128)} %bitcast.11, s32[1,3,1,8]{3,2,1,0:T(1,128)} %bitcast.12, bf16[3,8,64,256]{3,2,1,0:T(8,128)(2,1)} %bitcast.8, bf16[3,8,64,256]{3,2,1,0:T(8,128)(2,1)} %bitcast.9, bf16[27,256,256]{2,1,0:T(8,128)(2,1)} %w_hbm.1, ...), custom_call_target="tpu_custom_call" | custom-call | tf_op jit(solution)/shard_map/backward/pallas_call | solution.py:437
  67.7 5.9 %final.1 = (bf16[24,8,64,128]{3,2,1,0:T(8,128)(2,1)}, f32[864,256]{1,0:T(8,128)}, f32[128,256]{1,0:T(8,128)}) custom-call(bf16[24,64,256]{2,1,0:T(8,128)(2,1)} %get-tuple-element.9.refs_0_, bf16[1024,256]{1,0:T(8,128)(2,1)} %bitcast.10, bf16[864,256]{1,0:T(8,128)(2,1)} %get-tuple-element.10.refs_2_, bf16[128,256]{1,0:T(8,128)(2,1)} %get-tuple-element.11.refs_3_), custom_call_target="tpu_custom_call" | custom-call | tf_op jit(solution)/shard_map/final/pallas_call | solution.py:494

commit v4 on v3

--- a/solution.py
+++ b/solution.py
@@ -1,3 +1,4 @@
+import functools
 import math
 
 import jax
@@ -12,7 +13,15 @@
 F32 = jnp.float32
 CAP = 3
 GROUPS = 4
-FLOWS = ((2, 0, 256, "z"), (3, 0, 128, "y"), (3, 128, 128, "x"), (0, 0, 256, "x"), (1, 0, 128, "z"), (1, 128, 128, "y"))
+FLOWS = (
+    (2, 0, 256, "z"),
+    (3, 0, 128, "y"),
+    (0, 0, 256, "x"),
+    (1, 0, 128, "y"),
+    (1, 128, 128, "z"),
+    (3, 128, 128, "x"),
+)
+SPLIT = (9, 10, 13, 16, 2, 3, 6, 19, 20, 23, 26)
 
 
 def dot_nt(a, b):
@@ -24,11 +33,11 @@
 
 
 def kernel(
-    links, routes, g_hbm, p_hbm, w_hbm, fine_hbm,
-    octin_hbm, conv_hbm, down_hbm,
-    g, p, face, pface, gsh, ash, gt, w, fine, acc, octs, out, octin, ot,
-    part, rcore, racc, r1, s1, a1, r2, red, conv,
-    load_sem, halo_s, halo_r, oct_s, oct_r, red_s, red_r, put_sem,
+    scale, links, routes, g_hbm, p_hbm, w_hbm, dw_hbm, fine_hbm,
+    fg, conv, down_out,
+    g, p, face, pface, gsh, ash, gt, w, dw, fine, acc, octs, out, octin, ot,
+    part, rcore, racc, r1, s1, a1, r2, red,
+    load_sem, halo_s, halo_r, oct_s, oct_r, red_s, red_r,
 ):
     dp = lax.axis_index("dp")
     dom = lax.axis_index("dom")
@@ -56,7 +65,7 @@
 
     loads = []
     for i, (src, dst) in enumerate(
-        ((g_hbm, g.at[0:CAP]), (p_hbm, p.at[0:CAP]), (w_hbm, w), (fine_hbm, fine))
+        ((g_hbm, g.at[0:CAP]), (p_hbm, p.at[0:CAP]), (w_hbm, w), (fine_hbm, fine), (dw_hbm, dw))
     ):
         c = pltpu.make_async_copy(src, dst, load_sem.at[i])
         c.start()
@@ -68,7 +77,7 @@
         pface[i, CAP] = jnp.zeros(face.shape[2:], BF)
     octs[24] = jnp.zeros(octs.shape[1:], BF)
     for s in range(8):
-        part[3, s // 2, s % 2, 3, 2:4] = jnp.zeros((2, 16, 256), BF)
+        part[3, s // 2, s % 2, 3, :, :, 0:128] = jnp.zeros((4, 16, 128), BF)
     loads[0].wait()
     loads[1].wait()
 
@@ -187,39 +196,24 @@
             passing.append(c)
         place(1)
 
-    acc[...] = jnp.zeros(acc.shape, F32)
-    lax.fori_loop(0, CAP * 8, inner_g, 0)
+    lax.fori_loop(0, CAP * 8, inner_p, 0)
     pl.semaphore_wait(barrier, len(peers))
 
     halos = []
     for i, (src, dst, to) in enumerate(
         (
+            (p.at[0:CAP, 7], pface.at[0], nxt),
+            (p.at[0:CAP, 0], pface.at[1], prv),
             (g.at[0:CAP, 7], face.at[0], nxt),
             (g.at[0:CAP, 0], face.at[1], prv),
-            (p.at[0:CAP, 7], pface.at[0], nxt),
-            (p.at[0:CAP, 0], pface.at[1], prv),
         )
     ):
         c = rcopy(src, dst.at[0:CAP], halo_s.at[i], halo_r.at[i], to)
         c.start()
         halos.append(c)
 
-    loads[2].wait()
-    input_grad(0, 3, 6)
-    input_grad(1, 3, 6)
-    halos[0].wait_recv()
-    halos[1].wait_recv()
-    lax.fori_loop(0, CAP, outer_g, 0)
-    for half in range(2):
-        input_grad(half, 0, 3)
-        input_grad(half, 6, 9)
-        octants(half)
-        route(half)
-
-    lax.fori_loop(0, CAP * 8, inner_p, 0)
-    halos[2].wait_recv()
-    halos[3].wait_recv()
-    lax.fori_loop(0, CAP, outer_p, 0)
+    lax.fori_loop(0, CAP * 8, inner_g, 0)
+    acc[...] = jnp.zeros(acc.shape, F32)
 
     def transpose_plane(x, _):
         gt[:, pl.ds(pl.multiple_of(x * 384, 384), 384)] = (
@@ -241,20 +235,20 @@
 
         return one
 
-    def split_tap(n, _):
-        t = 2 + n
-        for at, jump in ((2, 2), (3, 2), (5, 2), (6, 2), (7, 2), (9, 2), (10, 2)):
-            t = t + jnp.where(n >= at, jump, 0)
+    def split_tap(t):
         grad = tap(t)
         for i in range(8):
-            m = t * 8 + i
-            k, r = m // 27, m % 27
-            pos = jnp.where(t < (27 * k + 7) // 8, r, r - 16)
-            q8 = pos % 8
-            part[2 + pos // 8, k // 2, k % 2, q8 // 2, pl.ds((q8 % 2) * 2, 2)] = grad[
-                32 * i : 32 * i + 32
-            ].reshape(2, 16, 256)
-        return 0
+            k, r = divmod(8 * t + i, 27)
+            pos = r if t < (27 * k + 7) // 8 else r - 16
+            rows = grad[32 * i : 32 * i + 32]
+            if pos < 8:
+                y = pos % 2 * 2
+                part[2, k // 2, k % 2, pos // 2, y : y + 2] = rows.reshape(2, 16, 256)
+            else:
+                for n in range(4):
+                    part[3, k // 2, k % 2, pos - 8, n, :, 0:128] = rows[
+                        n // 2 * 16 : n // 2 * 16 + 16, n % 2 * 128 : n % 2 * 128 + 128
+                    ]
 
     def cut(ref, axis, at):
         return ref.at[tuple(at if d == axis else slice(None) for d in "zxy")]
@@ -346,27 +340,55 @@
             self.all_of(8).wait_send()
 
     flows = [Flow(i) for i in range(len(FLOWS))]
-    fc, fa = flows[0:1], flows[3:4]
-    fd, fb = flows[1:3], flows[4:6]
+    fc, fa, fb, fd = flows[0:2], flows[2:3], flows[3:5], flows[5:6]
 
     def step(*some):
         for group in some:
             for one in group:
                 one.step()
 
-    lax.fori_loop(0, 11, split_tap, 0)
+    for t in SPLIT[:4]:
+        split_tap(t)
+    halos[0].wait_recv()
+    halos[1].wait_recv()
+    lax.fori_loop(0, CAP, outer_p, 0)
+    for t in SPLIT[4:]:
+        split_tap(t)
     step(fc)
+    lax.fori_loop(0, 8, whole_tap(0), 0)
+    step(fa, fc)
+    halos[2].wait_recv()
+    halos[3].wait_recv()
+    lax.fori_loop(0, CAP, outer_g, 0)
+    loads[2].wait()
+    input_grad(0, 0, 5)
+    step(fa, fc)
+    input_grad(0, 5, 9)
+    octants(0)
+    route(0)
+    step(fa, fc)
+    input_grad(1, 0, 5)
+    step(fa, fc)
+    input_grad(1, 5, 9)
+    octants(1)
+    route(1)
+    step(fa, fc)
+    lax.fori_loop(0, 8, whole_tap(1), 0)
+    step(fb, fa)
+    loads[4].wait()
+
+    def fine_grad(i, _):
+        at = pl.ds(4 * i, 4)
+        res = dot_nt(octin[at].reshape(256, 256), dw[...]).astype(BF)
+        for q in range(8):
+            fg[at, q] = res[:, 128 * q : 128 * q + 128].reshape(4, 64, 128)
+        return 0
+
+    lax.fori_loop(2, 4, fine_grad, 0)
+    loads[3].wait()
+    step(fb)
     for c in passing:
         c.wait_recv()
-    puts = []
-
-    def put(src, dst):
-        c = pltpu.make_async_copy(src, dst, put_sem.at[len(puts)])
-        c.start()
-        puts.append(c)
-
-    put(octin, octin_hbm)
-    loads[3].wait()
 
     def turn(i, _):
         ot[:, pl.ds(pl.multiple_of(i * 384, 384), 384)] = (
@@ -383,50 +405,46 @@
         grad = dot_nn(ot[...], rows).T.astype(BF)
         for c in range(2):
             one = grad[128 * c : 128 * c + 128]
-            part[3, i, c, 1, 2:4] = one[0:32].reshape(2, 16, 256)
-            part[3, i, c, 2] = one[32:96].reshape(4, 16, 256)
-            part[3, i, c, 3, 0:2] = one[96:128].reshape(2, 16, 256)
+            for n in range(16):
+                part[3, i, c, n // 4, n % 4, :, 128:256] = one[
+                    n // 2 * 16 : n // 2 * 16 + 16, n % 2 * 128 : n % 2 * 128 + 128
+                ]
         return 0
 
     lax.fori_loop(0, 4, down, 0)
-    step(fd, fc)
-    lax.fori_loop(0, 4, whole_tap(0), 0)
+    step(fd, fb)
+
+    lead = (27 * dp + 7) // 8 * 8 - 27 * dp
+    start = pl.multiple_of(lead * 32, 32)
+
+    def finished(value):
+        return value.astype(F32) * scale
+
+    conv[pl.ds(start, 256)] = finished(red[0].reshape(256, 256))
+    for n in range(11):
+        row = pl.multiple_of(32 * (n + jnp.where(n < lead, 0, 16)), 32)
+        if n < 8:
+            piece = red[2, n // 2, (n % 2) * 2 : (n % 2) * 2 + 2]
+            conv[pl.ds(row, 32)] = finished(piece.reshape(32, 256))
+        else:
+            for m in range(4):
+                conv[pl.ds(row + m // 2 * 16, 16), m % 2 * 128 : m % 2 * 128 + 128] = finished(
+                    red[3, n - 8, m, :, 0:128]
+                )
+    lax.fori_loop(0, 2, fine_grad, 0)
+    step(fd, fb)
+    lax.fori_loop(4, 6, fine_grad, 0)
+    step(fd, fb, fd, fb, fd)
+    conv[pl.ds(start + 256, 256)] = finished(red[1].reshape(256, 256))
     step(fd)
-    lax.fori_loop(4, 8, whole_tap(0), 0)
-    step(fa, fc)
-    lax.fori_loop(0, 4, whole_tap(1), 0)
-    step(fa, fd, fc)
-    lax.fori_loop(4, 8, whole_tap(1), 0)
-    step(fb, fa, fd, fb, fc, fa, fd, fb, fc, fb, fa, fd, fb, fa, fb)
-
-    k = dp
-    lead = (27 * k + 7) // 8 * 8 - 27 * k
-    start = pl.multiple_of(lead * 32, 32)
-    conv[pl.ds(start, 256)] = red[0].reshape(256, 256)
-    conv[pl.ds(start + 256, 256)] = red[1].reshape(256, 256)
-    for n in range(11):
-        row = 32 * (n + jnp.where(n < lead, 0, 16))
-        piece = red[2 + n // 8, n % 8 // 2, (n % 2) * 2 : (n % 2) * 2 + 2]
-        conv[pl.ds(pl.multiple_of(row, 32), 32)] = piece.reshape(32, 256)
-    conv[864:896] = red[3, 1, 2:4].reshape(32, 256)
-    conv[896:960] = red[3, 2].reshape(64, 256)
-    conv[960:992] = red[3, 3, 0:2].reshape(32, 256)
-    put(conv.at[0:864], conv_hbm)
-    put(conv.at[864:992], down_hbm)
+    for n in range(16):
+        down_out[n // 2 * 16 : n // 2 * 16 + 16, n % 2 * 128 : n % 2 * 128 + 128] = finished(
+            red[3, n // 4, n % 4, :, 128:256]
+        )
     for c in halos + passing:
         c.wait_send()
     for one in flows:
         one.finish()
-    for c in puts:
-        c.wait()
-
-
-def final(scale, octin, dw, conv_in, down_in, fg, conv, down):
-    res = dot_nt(octin[...].reshape(256, 256), dw[...]).astype(BF)
-    for q in range(8):
-        fg[:, q] = res[:, 128 * q : 128 * q + 128].reshape(4, 64, 128)
-    conv[...] = conv_in[...].astype(F32) * scale
-    down[...] = down_in[...].astype(F32) * scale
 
 
 def body(grad_out, pre_act, conv_weight, down_weight, fine_act, neighbours, octant_routes):
@@ -434,15 +452,13 @@
     any_space = pl.BlockSpec(memory_space=pl.ANY)
     smem = pl.BlockSpec(memory_space=pltpu.SMEM)
     V = pltpu.VMEM
-    octin, conv, down = pl.pallas_call(
-        kernel,
-        out_shape=(
-            jax.ShapeDtypeStruct((24, 64, 256), BF),
-            jax.ShapeDtypeStruct((864, 256), BF),
-            jax.ShapeDtypeStruct((128, 256), BF),
-        ),
-        in_specs=[smem, smem] + [any_space] * 4,
-        out_specs=(any_space, any_space, any_space),
+    factor = 1.0 / math.sqrt(lax.axis_size("dp") * lax.axis_size("dom") * slots * voxels)
+    vmem = pl.BlockSpec(memory_space=V)
+    fg, conv, down = pl.pallas_call(
+        functools.partial(kernel, factor),
+        out_shape=(V((24, 8, 64, 128), BF), V((864, 256), F32), V((128, 256), F32)),
+        in_specs=[smem, smem] + [any_space] * 5,
+        out_specs=(vmem, vmem, vmem),
         scratch_shapes=[
             V((CAP + 1, 8, 64, 256), BF),
             V((CAP + 1, 8, 64, 256), BF),
@@ -452,6 +468,7 @@
             V((9, 10, 192, 256), BF),
             V((256, 1536), BF),
             V((27, 256, 256), BF),
+            V((1024, 256), BF),
             V((24, 8, 64, 128), BF),
             V((2, 768, 256), F32),
             V((25, 64, 256), BF),
@@ -466,18 +483,16 @@
             V((GROUPS, 4, 4, 16, 256), BF),
             V((GROUPS, 15, 16, 256), BF),
             V((GROUPS, 4, 4, 16, 256), BF),
-            V((992, 256), BF),
-            pltpu.SemaphoreType.DMA((4,)),
+            pltpu.SemaphoreType.DMA((5,)),
             pltpu.SemaphoreType.DMA((4,)),
             pltpu.SemaphoreType.DMA((4,)),
             pltpu.SemaphoreType.DMA((4,)),
             pltpu.SemaphoreType.DMA((4,)),
             pltpu.SemaphoreType.DMA((len(FLOWS), 9)),
             pltpu.SemaphoreType.DMA((len(FLOWS), 9)),
-            pltpu.SemaphoreType.DMA((3,)),
         ],
         compiler_params=pltpu.CompilerParams(
-            collective_id=0, has_side_effects=True, vmem_limit_bytes=60 * 1024 * 1024
+            collective_id=0, has_side_effects=True, vmem_limit_bytes=54 * 1024 * 1024
         ),
         name="backward",
     )(
@@ -486,28 +501,9 @@
         grad_out[0].reshape(slots, 8, 64, channels),
         pre_act[0].reshape(slots, 8, 64, channels),
         conv_weight,
+        down_weight.reshape(1024, 256),
         fine_act[0].reshape(24, 8, 64, 128),
     )
-    factor = 1.0 / math.sqrt(lax.axis_size("dp") * lax.axis_size("dom") * slots * voxels)
-    whole = pl.BlockSpec((128, 256), lambda i: (0, 0))
-    rows = pl.BlockSpec((144, 256), lambda i: (i, 0))
-    fg, conv, down = pl.pallas_call(
-        lambda *refs: final(factor, *refs),
-        out_shape=(
-            jax.ShapeDtypeStruct((24, 8, 64, 128), BF),
-            jax.ShapeDtypeStruct((864, 256), F32),
-            jax.ShapeDtypeStruct((128, 256), F32),
-        ),
-        grid=(6,),
-        in_specs=[
-            pl.BlockSpec((4, 64, 256), lambda i: (i, 0, 0)),
-            pl.BlockSpec((1024, 256), lambda i: (0, 0)),
-            rows,
-            whole,
-        ],
-        out_specs=(pl.BlockSpec((4, 8, 64, 128), lambda i: (i, 0, 0, 0)), rows, whole),
-        name="final",
-    )(octin, down_weight.reshape(1024, 256), conv, down)
     return (fg.reshape(fine_act.shape), conv, down)
 
 

time: 73.9 us -> 74.3 us (level)
  local copies, waits for them, and re-layouts: 0 us -> 3.23 us
  Pallas kernels: 73 us -> 70.3 us
    unnamed x0 -> x3, local copies, waits for them, and re-layouts: none -> 3.23 us
    pallas_call x2 -> x1, Pallas kernels: 73 us -> 70.3 us  [body(): pl.pallas_call(functools.partial(kernel, factor), out_shape=(V((24, 8, 64...]
where the time goes in v4:
time: 74.3 us; the launch traced here: 74.2 us
  Pallas kernels  70.3 us (95%)
  local copies, waits for them, and re-layouts  3.23 us (4%)
    pallas_call x1, Pallas kernels, body(): pl.pallas_call(functools.partial(kernel, factor), out_shape=(V((24, 8, 64...  70.3 us
    unnamed x3, local copies, waits for them, and re-layouts  3.23 us

profile of v4, /device:TPU:0, one launch (start us, length us, event | category | flops | bytes accessed | tf_op | source)
XLA Modules:
  0.0 74.2 jit_solution(14024844914562955840)
XLA Ops:
  0.6 70.3 %backward.1 = (bf16[24,8,64,128]{3,2,1,0:T(8,128)(2,1)S(1)}, f32[864,256]{1,0:T(8,128)S(1)}, f32[128,256]{1,0:T(8,128)S(1)}) custom-call(s32[3,1,27]{2,1,0:T(1,128)} %bitcast.12, s32[1,3,1,8]{3,2,1,0:T(1,128)} %bitcast.13, bf16[3,8,64,256]{3,2,1,0:T(8,128)(2,1)} %bitcast.9, bf16[3,8,64,256]{3,2,1,0:T(8,128)(2,1)} %bitcast.10, bf16[27,256,256]{2,1,0:T(8,128)(2,1)} %w_hbm.1, ...), custom_call_target="tpu_custom_call" | custom-call | tf_op jit(solution)/shard_map/backward/pallas_call | solution.py:457
  70.9 1.7 %copy.13 = bf16[1,24,512,128]{3,2,1,0:T(8,128)(2,1)} copy(bf16[1,24,512,128]{3,2,1,0:T(8,128)(2,1)S(1)} %bitcast.7) | data formatting | bytes 6291456
  72.6 0.7 copy.15
  73.2 0.9 %copy.14 = f32[864,256]{1,0:T(8,128)} copy(f32[864,256]{1,0:T(8,128)S(1)} %get-tuple-element.10) | data formatting | bytes 1769472

commit v5 on v4

--- a/solution.py
+++ b/solution.py
@@ -16,7 +16,7 @@
 FLOWS = (
     (2, 0, 256, "z"),
     (3, 0, 128, "y"),
-    (0, 0, 256, "x"),
+    (0, 0, 256, "z"),
     (1, 0, 128, "y"),
     (1, 128, 128, "z"),
     (3, 128, 128, "x"),
@@ -36,7 +36,7 @@
     scale, links, routes, g_hbm, p_hbm, w_hbm, dw_hbm, fine_hbm,
     fg, conv, down_out,
     g, p, face, pface, gsh, ash, gt, w, dw, fine, acc, octs, out, octin, ot,
-    part, rcore, racc, r1, s1, a1, r2, red,
+    part, rcore, racc, r1, a1, r2, red,
     load_sem, halo_s, halo_r, oct_s, oct_r, red_s, red_r,
 ):
     dp = lax.axis_index("dp")
@@ -262,82 +262,60 @@
             self.rcore = rcore.at[grp, :, :, :, :, lanes]
             self.racc = racc.at[grp, :, :, :, :, lanes]
             self.r1 = r1.at[grp, :, :, :, :, lanes]
-            self.s1 = s1.at[grp, :, :, :, :, lanes]
             self.a1 = a1.at[grp, :, :, :, lanes]
             self.r2 = r2.at[grp, :, :, lanes]
             self.red = red.at[grp, :, :, :, lanes]
             self.stage = 0
-            self.sends = []
 
         def send(self, src, dst, i, to):
             c = rcopy(src, dst, red_s.at[self.n, i], red_r.at[self.n, i], to)
             c.start()
-            if i < 7:
-                self.sends.append(c)
             return c
 
         def all_of(self, i):
-            return rcopy(self.r2, self.r2, red_s.at[self.n, i], red_r.at[self.n, i], partner)
-
-        def chunk(self, off, half):
-            ref = cut(self.racc, self.axis, lax.rem(coord[self.axis] + off, 4))
-            return ref.at[2 * half : 2 * half + 2]
+            ref = (self.rcore, self.r1, self.r2, self.r2)[i]
+            return rcopy(ref, ref, red_s.at[self.n, i], red_r.at[self.n, i], partner)
+
+        def chunk(self, off):
+            return cut(self.racc, self.axis, lax.rem(coord[self.axis] + off, 4))
 
         def step(self):
             axis = self.axis
-            left, right = at_offset(**{axis: 3}), at_offset(**{axis: 1})
             u, v = "zxy".replace(axis, "")
             stage = self.stage
             self.stage += 1
+            if stage > 0:
+                self.all_of(stage - 1).wait_recv()
             if stage == 0:
-                self.core = self.send(self.part.at[:, 1 - cc], self.rcore, 0, partner)
+                self.send(self.part.at[:, 1 - cc], self.rcore, 0, partner)
             elif stage == 1:
-                self.core.wait_recv()
                 for z in range(4):
                     self.racc[z] = (
                         self.part[z, cc].astype(F32) + self.rcore[z].astype(F32)
                     ).astype(BF)
-                box = self.r1
-                self.relay_a = self.send(self.chunk(2, 0), box.at[0], 1, right)
-                self.relay_b = self.send(self.chunk(2, 1), box.at[1], 2, left)
-                self.direct_b = self.send(self.chunk(1, 1), box.at[2], 3, right)
-                self.direct_a = self.send(self.chunk(3, 0), box.at[3], 4, left)
+                for off in (2, 1, 3):
+                    self.send(self.chunk(off), self.r1.at[off - 1], 1, at_offset(**{axis: off}))
             elif stage == 2:
-                box = self.r1
-                self.relay_a.wait_recv()
-                self.s1[0] = (self.chunk(1, 0)[...].astype(F32) + box[0].astype(F32)).astype(BF)
-                self.sum_a = self.send(self.s1.at[0], box.at[4], 5, right)
-                self.relay_b.wait_recv()
-                self.s1[1] = (self.chunk(3, 1)[...].astype(F32) + box[1].astype(F32)).astype(BF)
-                self.sum_b = self.send(self.s1.at[1], box.at[5], 6, left)
-            elif stage == 3:
-                for c in (self.direct_a, self.direct_b, self.sum_a, self.sum_b):
-                    c.wait_recv()
-                for half, (i, j) in enumerate(((4, 3), (5, 2))):
-                    total = self.chunk(0, half)[...].astype(F32)
-                    total = total + self.r1[i].astype(F32) + self.r1[j].astype(F32)
-                    self.a1[2 * half : 2 * half + 2] = total.astype(BF)
+                total = self.chunk(0)[...].astype(F32)
+                for n in range(3):
+                    total = total + self.r1[n].astype(F32)
+                self.a1[...] = total.astype(BF)
                 for n in range(1, 16):
                     du, dv = n // 4, n % 4
                     src = self.a1.at[lax.rem(coord[u] + du, 4), lax.rem(coord[v] + dv, 4)]
-                    self.send(src, self.r2.at[n - 1], 7, at_offset(**{u: du, v: dv}))
-            elif stage == 4:
-                self.all_of(7).wait_recv()
+                    self.send(src, self.r2.at[n - 1], 2, at_offset(**{u: du, v: dv}))
+            elif stage == 3:
                 total = self.a1[coord[u], coord[v]].astype(F32)
                 for n in range(15):
                     total = total + self.r2[n].astype(F32)
                 self.red[xc, yc] = total.astype(BF)
                 spot = self.red.at[xc, yc]
                 for n in range(1, 16):
-                    self.send(spot, spot, 8, at_offset(x=n // 4, y=n % 4))
-            else:
-                self.all_of(8).wait_recv()
+                    self.send(spot, spot, 3, at_offset(x=n // 4, y=n % 4))
 
         def finish(self):
-            for c in self.sends:
-                c.wait_send()
-            self.all_of(7).wait_send()
-            self.all_of(8).wait_send()
+            for i in range(4):
+                self.all_of(i).wait_send()
 
     flows = [Flow(i) for i in range(len(FLOWS))]
     fc, fa, fb, fd = flows[0:2], flows[2:3], flows[3:5], flows[5:6]
@@ -355,26 +333,23 @@
     for t in SPLIT[4:]:
         split_tap(t)
     step(fc)
-    lax.fori_loop(0, 8, whole_tap(0), 0)
-    step(fa, fc)
     halos[2].wait_recv()
     halos[3].wait_recv()
     lax.fori_loop(0, CAP, outer_g, 0)
     loads[2].wait()
     input_grad(0, 0, 5)
-    step(fa, fc)
+    step(fc)
     input_grad(0, 5, 9)
     octants(0)
     route(0)
-    step(fa, fc)
-    input_grad(1, 0, 5)
-    step(fa, fc)
-    input_grad(1, 5, 9)
+    input_grad(1, 0, 9)
     octants(1)
     route(1)
-    step(fa, fc)
+    step(fc)
+    lax.fori_loop(0, 8, whole_tap(0), 0)
+    step(fa)
     lax.fori_loop(0, 8, whole_tap(1), 0)
-    step(fb, fa)
+    step(fb, fa, fc)
     loads[4].wait()
 
     def fine_grad(i, _):
@@ -386,9 +361,9 @@
 
     lax.fori_loop(2, 4, fine_grad, 0)
     loads[3].wait()
-    step(fb)
     for c in passing:
         c.wait_recv()
+    step(fb)
 
     def turn(i, _):
         ot[:, pl.ds(pl.multiple_of(i * 384, 384), 384)] = (
@@ -412,7 +387,10 @@
         return 0
 
     lax.fori_loop(0, 4, down, 0)
-    step(fd, fb)
+    step(fd)
+    lax.fori_loop(0, 2, fine_grad, 0)
+    lax.fori_loop(4, 6, fine_grad, 0)
+    step(fa, fc, fd)
 
     lead = (27 * dp + 7) // 8 * 8 - 27 * dp
     start = pl.multiple_of(lead * 32, 32)
@@ -420,7 +398,6 @@
     def finished(value):
         return value.astype(F32) * scale
 
-    conv[pl.ds(start, 256)] = finished(red[0].reshape(256, 256))
     for n in range(11):
         row = pl.multiple_of(32 * (n + jnp.where(n < lead, 0, 16)), 32)
         if n < 8:
@@ -431,10 +408,9 @@
                 conv[pl.ds(row + m // 2 * 16, 16), m % 2 * 128 : m % 2 * 128 + 128] = finished(
                     red[3, n - 8, m, :, 0:128]
                 )
-    lax.fori_loop(0, 2, fine_grad, 0)
+    step(fb, fa, fd, fb, fa)
+    conv[pl.ds(start, 256)] = finished(red[0].reshape(256, 256))
     step(fd, fb)
-    lax.fori_loop(4, 6, fine_grad, 0)
-    step(fd, fb, fd, fb, fd)
     conv[pl.ds(start + 256, 256)] = finished(red[1].reshape(256, 256))
     step(fd)
     for n in range(16):
@@ -478,8 +454,7 @@
             V((GROUPS, 4, 2, 4, 4, 16, 256), BF),
             V((GROUPS, 4, 4, 4, 16, 256), BF),
             V((GROUPS, 4, 4, 4, 16, 256), BF),
-            V((GROUPS, 6, 2, 4, 16, 256), BF),
-            V((GROUPS, 2, 2, 4, 16, 256), BF),
+            V((GROUPS, 3, 4, 4, 16, 256), BF),
             V((GROUPS, 4, 4, 16, 256), BF),
             V((GROUPS, 15, 16, 256), BF),
             V((GROUPS, 4, 4, 16, 256), BF),
@@ -488,8 +463,8 @@
             pltpu.SemaphoreType.DMA((4,)),
             pltpu.SemaphoreType.DMA((4,)),
             pltpu.SemaphoreType.DMA((4,)),
-            pltpu.SemaphoreType.DMA((len(FLOWS), 9)),
-            pltpu.SemaphoreType.DMA((len(FLOWS), 9)),
+            pltpu.SemaphoreType.DMA((len(FLOWS), 4)),
+            pltpu.SemaphoreType.DMA((len(FLOWS), 4)),
         ],
         compiler_params=pltpu.CompilerParams(
             collective_id=0, has_side_effects=True, vmem_limit_bytes=54 * 1024 * 1024

time: 74.3 us -> 64.7 us (0.87)
  Pallas kernels: 70.3 us -> 60.7 us
    pallas_call x1, Pallas kernels: 70.3 us -> 60.7 us  [body(): pl.pallas_call(functools.partial(kernel, factor), out_shape=(V((24, 8, 64...]
where the time goes in v5:
time: 64.7 us; the launch traced here: 64.6 us
  Pallas kernels  60.7 us (94%)
  local copies, waits for them, and re-layouts  3.23 us (5%)
    pallas_call x1, Pallas kernels, body(): pl.pallas_call(functools.partial(kernel, factor), out_shape=(V((24, 8, 64...  60.7 us
    unnamed x3, local copies, waits for them, and re-layouts  3.23 us

profile of v5, /device:TPU:0, one launch (start us, length us, event | category | flops | bytes accessed | tf_op | source)
XLA Modules:
  0.0 64.6 jit_solution(4864613137521472962)
XLA Ops:
  0.6 60.7 %backward.1 = (bf16[24,8,64,128]{3,2,1,0:T(8,128)(2,1)S(1)}, f32[864,256]{1,0:T(8,128)S(1)}, f32[128,256]{1,0:T(8,128)S(1)}) custom-call(s32[3,1,27]{2,1,0:T(1,128)} %bitcast.12, s32[1,3,1,8]{3,2,1,0:T(1,128)} %bitcast.13, bf16[3,8,64,256]{3,2,1,0:T(8,128)(2,1)} %bitcast.9, bf16[3,8,64,256]{3,2,1,0:T(8,128)(2,1)} %bitcast.10, bf16[27,256,256]{2,1,0:T(8,128)(2,1)} %w_hbm.1, ...), custom_call_target="tpu_custom_call" | custom-call | tf_op jit(solution)/shard_map/backward/pallas_call | solution.py:433
  61.4 1.7 %copy.13 = bf16[1,24,512,128]{3,2,1,0:T(8,128)(2,1)} copy(bf16[1,24,512,128]{3,2,1,0:T(8,128)(2,1)S(1)} %bitcast.7) | data formatting | bytes 6291456
  63.0 0.7 %copy.15 = f32[128,256]{1,0:T(8,128)} copy(f32[128,256]{1,0:T(8,128)S(1)} %get-tuple-element.11) | data formatting | bytes 262144
  63.7 0.9 %copy.14 = f32[864,256]{1,0:T(8,128)} copy(f32[864,256]{1,0:T(8,128)S(1)} %get-tuple-element.10) | data formatting | bytes 1769472

commit v6 on v5

--- a/solution.py
+++ b/solution.py
@@ -16,10 +16,10 @@
 FLOWS = (
     (2, 0, 256, "z"),
     (3, 0, 128, "y"),
-    (0, 0, 256, "z"),
-    (1, 0, 128, "y"),
+    (0, 0, 256, "y"),
+    (1, 0, 128, "x"),
     (1, 128, 128, "z"),
-    (3, 128, 128, "x"),
+    (3, 128, 128, "y"),
 )
 SPLIT = (9, 10, 13, 16, 2, 3, 6, 19, 20, 23, 26)
 
@@ -133,16 +133,10 @@
         return 0
 
     def input_grad(half, first, last):
-        def taps(n, _):
-            tx, ty = n // 3, n % 3
-            lhs = jnp.concatenate(
-                [
-                    gsh[8 - 3 * ty - tz, pl.ds(2 - tx + 4 * half, 4)].reshape(768, 256)
-                    for tz in range(3)
-                ],
-                axis=1,
-            )
-            rhs = jnp.concatenate([w[3 * n + tz] for tz in range(3)], axis=1)
+        def taps(tx, _):
+            rows = pl.ds(2 - tx + 4 * half, 4)
+            lhs = jnp.concatenate([gsh[8 - n, rows].reshape(768, 256) for n in range(9)], axis=1)
+            rhs = jnp.concatenate([w[9 * tx + n] for n in range(9)], axis=1)
             acc[half] += dot_nt(lhs, rhs)
             return 0
 
@@ -229,8 +223,13 @@
         return dot_nn(gt[...], rows).T.astype(BF)
 
     def whole_tap(shift):
-        def one(k, _):
-            part[shift, k // 2, k % 2] = tap((27 * k + 7) // 8 + shift).reshape(4, 4, 16, 256)
+        def one(z, _):
+            rows = []
+            for c in range(2):
+                t = (27 * (2 * z + c) + 7) // 8 + shift
+                rows.append(ash[t % 9, pl.ds(t // 9, 8)].reshape(1536, 256))
+            grad = dot_nn(gt[...], jnp.concatenate(rows, axis=1)).T.astype(BF)
+            part[shift, z] = grad.reshape(2, 4, 4, 16, 256)
             return 0
 
         return one
@@ -333,23 +332,23 @@
     for t in SPLIT[4:]:
         split_tap(t)
     step(fc)
+    lax.fori_loop(0, 4, whole_tap(0), 0)
+    step(fa)
     halos[2].wait_recv()
     halos[3].wait_recv()
     lax.fori_loop(0, CAP, outer_g, 0)
     loads[2].wait()
-    input_grad(0, 0, 5)
+    input_grad(0, 0, 2)
     step(fc)
-    input_grad(0, 5, 9)
+    input_grad(0, 2, 3)
+    step(fa)
     octants(0)
     route(0)
-    input_grad(1, 0, 9)
+    input_grad(1, 0, 3)
     octants(1)
     route(1)
-    step(fc)
-    lax.fori_loop(0, 8, whole_tap(0), 0)
-    step(fa)
-    lax.fori_loop(0, 8, whole_tap(1), 0)
-    step(fb, fa, fc)
+    lax.fori_loop(0, 4, whole_tap(1), 0)
+    step(fb)
     loads[4].wait()
 
     def fine_grad(i, _):
@@ -387,10 +386,10 @@
         return 0
 
     lax.fori_loop(0, 4, down, 0)
-    step(fd)
+    step(fd, fc, fa)
     lax.fori_loop(0, 2, fine_grad, 0)
     lax.fori_loop(4, 6, fine_grad, 0)
-    step(fa, fc, fd)
+    step(fd, fb)
 
     lead = (27 * dp + 7) // 8 * 8 - 27 * dp
     start = pl.multiple_of(lead * 32, 32)
@@ -398,6 +397,7 @@
     def finished(value):
         return value.astype(F32) * scale
 
+    step(fc, fa, fd, fb, fc)
     for n in range(11):
         row = pl.multiple_of(32 * (n + jnp.where(n < lead, 0, 16)), 32)
         if n < 8:
@@ -408,7 +408,7 @@
                 conv[pl.ds(row + m // 2 * 16, 16), m % 2 * 128 : m % 2 * 128 + 128] = finished(
                     red[3, n - 8, m, :, 0:128]
                 )
-    step(fb, fa, fd, fb, fa)
+    step(fa)
     conv[pl.ds(start, 256)] = finished(red[0].reshape(256, 256))
     step(fd, fb)
     conv[pl.ds(start + 256, 256)] = finished(red[1].reshape(256, 256))

time: 64.7 us -> 59.7 us (0.923)
  Pallas kernels: 60.7 us -> 55.7 us
    pallas_call x1, Pallas kernels: 60.7 us -> 55.7 us  [body(): pl.pallas_call(functools.partial(kernel, factor), out_shape=(V((24, 8, 64...]
where the time goes in v6:
time: 59.7 us; the launch traced here: 59.5 us
  Pallas kernels  55.7 us (93%)
  local copies, waits for them, and re-layouts  3.23 us (5%)
  between operations  0.64 us (1%)
    pallas_call x1, Pallas kernels, body(): pl.pallas_call(functools.partial(kernel, factor), out_shape=(V((24, 8, 64...  55.7 us
    unnamed x3, local copies, waits for them, and re-layouts  3.23 us

profile of v6, /device:TPU:0, one launch (start us, length us, event | category | flops | bytes accessed | tf_op | source)
XLA Modules:
  0.0 59.5 jit_solution(6050513484234215004)
XLA Ops:
  0.6 55.7 %backward.1 = (bf16[24,8,64,128]{3,2,1,0:T(8,128)(2,1)S(1)}, f32[864,256]{1,0:T(8,128)S(1)}, f32[128,256]{1,0:T(8,128)S(1)}) custom-call(s32[3,1,27]{2,1,0:T(1,128)} %bitcast.12, s32[1,3,1,8]{3,2,1,0:T(1,128)} %bitcast.13, bf16[3,8,64,256]{3,2,1,0:T(8,128)(2,1)} %bitcast.9, bf16[3,8,64,256]{3,2,1,0:T(8,128)(2,1)} %bitcast.10, bf16[27,256,256]{2,1,0:T(8,128)(2,1)} %w_hbm.1, ...), custom_call_target="tpu_custom_call" | custom-call | tf_op jit(solution)/shard_map/backward/pallas_call | solution.py:433
  56.3 1.7 %copy.13 = bf16[1,24,512,128]{3,2,1,0:T(8,128)(2,1)} copy(bf16[1,24,512,128]{3,2,1,0:T(8,128)(2,1)S(1)} %bitcast.7) | data formatting | bytes 6291456
  58.0 0.7 %copy.15 = f32[128,256]{1,0:T(8,128)} copy(f32[128,256]{1,0:T(8,128)S(1)} %get-tuple-element.11) | data formatting | bytes 262144
  58.6 0.9 %copy.14 = f32[864,256]{1,0:T(8,128)} copy(f32[864,256]{1,0:T(8,128)S(1)} %get-tuple-element.10) | data formatting | bytes 1769472

commit v7 on v6

--- a/solution.py
+++ b/solution.py
@@ -21,6 +21,7 @@
     (1, 128, 128, "z"),
     (3, 128, 128, "y"),
 )
+FAR = sorted(range(1, 16), key=lambda n: -(min(n // 4, 4 - n // 4) + min(n % 4, 4 - n % 4)))
 SPLIT = (9, 10, 13, 16, 2, 3, 6, 19, 20, 23, 26)
 
 
@@ -299,7 +300,7 @@
                 for n in range(3):
                     total = total + self.r1[n].astype(F32)
                 self.a1[...] = total.astype(BF)
-                for n in range(1, 16):
+                for n in FAR:
                     du, dv = n // 4, n % 4
                     src = self.a1.at[lax.rem(coord[u] + du, 4), lax.rem(coord[v] + dv, 4)]
                     self.send(src, self.r2.at[n - 1], 2, at_offset(**{u: du, v: dv}))
@@ -309,7 +310,7 @@
                     total = total + self.r2[n].astype(F32)
                 self.red[xc, yc] = total.astype(BF)
                 spot = self.red.at[xc, yc]
-                for n in range(1, 16):
+                for n in FAR:
                     self.send(spot, spot, 3, at_offset(x=n // 4, y=n % 4))
 
         def finish(self):

time: 59.7 us -> 59.5 us (level)
  no operation moved by 1% of the time
where the time goes in v7:
time: 59.5 us; the launch traced here: 59.4 us
  Pallas kernels  55.5 us (93%)
  local copies, waits for them, and re-layouts  3.23 us (5%)
  between operations  0.64 us (1%)
    pallas_call x1, Pallas kernels, body(): pl.pallas_call(functools.partial(kernel, factor), out_shape=(V((24, 8, 64...  55.5 us
    unnamed x3, local copies, waits for them, and re-layouts  3.23 us

profile of v7, /device:TPU:0, one launch (start us, length us, event | category | flops | bytes accessed | tf_op | source)
XLA Modules:
  0.0 59.4 jit_solution(14172029036401698413)
XLA Ops:
  0.6 55.5 %backward.1 = (bf16[24,8,64,128]{3,2,1,0:T(8,128)(2,1)S(1)}, f32[864,256]{1,0:T(8,128)S(1)}, f32[128,256]{1,0:T(8,128)S(1)}) custom-call(s32[3,1,27]{2,1,0:T(1,128)} %bitcast.12, s32[1,3,1,8]{3,2,1,0:T(1,128)} %bitcast.13, bf16[3,8,64,256]{3,2,1,0:T(8,128)(2,1)} %bitcast.9, bf16[3,8,64,256]{3,2,1,0:T(8,128)(2,1)} %bitcast.10, bf16[27,256,256]{2,1,0:T(8,128)(2,1)} %w_hbm.1, ...), custom_call_target="tpu_custom_call" | custom-call | tf_op jit(solution)/shard_map/backward/pallas_call | solution.py:434
  56.2 1.7 %copy.13 = bf16[1,24,512,128]{3,2,1,0:T(8,128)(2,1)} copy(bf16[1,24,512,128]{3,2,1,0:T(8,128)(2,1)S(1)} %bitcast.7) | data formatting | bytes 6291456
  57.8 0.7 %copy.15 = f32[128,256]{1,0:T(8,128)} copy(f32[128,256]{1,0:T(8,128)S(1)} %get-tuple-element.11) | data formatting | bytes 262144
  58.5 0.9 %copy.14 = f32[864,256]{1,0:T(8,128)} copy(f32[864,256]{1,0:T(8,128)S(1)} %get-tuple-element.10) | data formatting | bytes 1769472
